TPU v7x, 32 devices: a whole 2x2x4 slice. The times are simulated.
32 devices in a mesh: wide: 16 (over z, y, core), narrow: 2 (over x).
Axes of the slice: x: 2, y: 2, z: 4, core: 2. Of those that a mesh axis runs over, the one named last changes fastest.
Arguments:
- tokens: bfloat16 [32, 256, 1120], P(('wide', 'narrow')), may hold values from -6 to 6
- lengths: int32 [32], P(('wide', 'narrow')), may hold values from 128 to 256
- dropped: int32 [32], P(('wide', 'narrow')), may hold values from 0 to 4
- cotangent: bfloat16 [32, 256, 1120], P(('wide', 'narrow')), may hold values from -6 to 6
- first_gain: bfloat16 [1120], P('narrow'), may hold values from 0.5 to 1.5
- first_shift: bfloat16 [1120], P('narrow'), may hold values from -1.5 to 1.5
- qkv_weight: bfloat16 [1120, 3360], P('narrow'), may hold values from -0.1875 to 0.1875
- query_bias: bfloat16 [1120], P('narrow'), may hold values from -2 to 2
- value_bias: bfloat16 [1120], P('narrow'), may hold values from -2 to 2
- out_weight: bfloat16 [1120, 1120], P('narrow'), may hold values from -1.5 to 1.5
- out_bias: bfloat16 [1120], P('narrow'), may hold values from -1.5 to 1.5
- second_gain: bfloat16 [1120], P('narrow'), may hold values from 0.5 to 1.5
- second_shift: bfloat16 [1120], P('narrow'), may hold values from -1.5 to 1.5
- up_weight: bfloat16 [1120, 4480], P('narrow'), may hold values from -0.1875 to 0.1875
- up_bias: bfloat16 [4480], P('narrow'), may hold values from -2 to 2
- down_weight: bfloat16 [4480, 1120], P('narrow'), may hold values from -0.1875 to 0.1875
- down_bias: bfloat16 [1120], P('narrow'), may hold values from -1.5 to 1.5
Outputs:
- output: bfloat16 [32, 256, 1120], P(('wide', 'narrow'))
- grad_tokens: float32 [32, 256, 1120], P(('wide', 'narrow'))
- grad_first_gain: float32 [1120], P('narrow')
- grad_first_shift: float32 [1120], P('narrow')
- grad_qkv_weight: float32 [1120, 3360], P('narrow', 'wide')
- grad_query_bias: float32 [1120], P('narrow')
- grad_value_bias: float32 [1120], P('narrow')
- grad_out_weight: float32 [1120, 1120], P('narrow', 'wide')
- grad_out_bias: float32 [1120], P('narrow')
- grad_second_gain: float32 [1120], P('narrow')
- grad_second_shift: float32 [1120], P('narrow')
- grad_up_weight: float32 [1120, 4480], P('narrow', 'wide')
- grad_up_bias: float32 [4480], P('narrow')
- grad_down_weight: float32 [4480, 1120], P('narrow', 'wide')
- grad_down_bias: float32 [1120], P('narrow')
All inputs are finite; a program needn't handle non-finite values.
Results may differ from a plain program's by a relative error of at most 0.018.
Values may be sent and summed in bfloat16 or wider, within the bound.
A program may use at most 192 MiB of HBM per device.

v0:
```python
import jax
import jax.numpy as jnp
from jax import lax
from jax.sharding import PartitionSpec as P

HEAD = 56
epsilon = 1e-05
head_groups = 4
AXES = ("wide", "narrow")
f32 = jnp.float32
bf16 = jnp.bfloat16


def dot(left, right):
    return jnp.dot(left, right, preferred_element_type=f32)


def tdot(left, right):
    return lax.dot_general(left, right, (((0,), (0,)), ((), ())), preferred_element_type=f32)


def dot_t(left, right):
    return lax.dot_general(left, right, (((1,), (1,)), ((), ())), preferred_element_type=f32)


def normed(values, gain, shift):
    center = values - jnp.mean(values, axis=-1, keepdims=True)
    spread = jnp.mean(center * center, axis=-1, keepdims=True)
    return center * lax.rsqrt(spread + epsilon) * gain + shift


def split_heads(matrix):
    rows = matrix.shape[0]
    return matrix.reshape(rows, head_groups, -1, HEAD).transpose(1, 0, 2, 3)


def join_heads(blocks):
    return blocks.transpose(1, 0, 2, 3).reshape(blocks.shape[1], -1)


def key_mask(length, drop, rows):
    places = jnp.arange(rows, dtype=jnp.int32)
    live = (places < length) & ((places < 1) | (places > drop))
    return (places[None, :] <= places[:, None]) & (
        live[None, :] | (places[None, :] == places[:, None])
    )


def scores_of(query, keys, mask):
    raw = jnp.einsum("qhe,khe->hqk", query, keys, preferred_element_type=f32) * HEAD ** (-0.5)
    return jnp.where(mask[None], raw, -jnp.inf)


def attention(query, keys, values, mask):

    def attend(group):
        scores = scores_of(group[0], group[1], mask)
        top = jnp.max(scores, axis=-1, keepdims=True)
        expos = jnp.exp(scores - top)
        total = jnp.sum(expos, axis=-1, keepdims=True)
        probs = (expos / total).astype(bf16)
        heads_out = jnp.einsum("hqk,khe->qhe", probs, group[2], preferred_element_type=f32)
        return (heads_out.astype(bf16), top + jnp.log(total))

    heads_out, logsum = lax.map(
        attend, (split_heads(query), split_heads(keys), split_heads(values))
    )
    return (join_heads(heads_out), logsum)


def attention_back(query, keys, values, logsum, d_attended, mask):

    def attend_back(group):
        q_part, k_part, v_part, lse_part, do_part = group
        scores = scores_of(q_part, k_part, mask)
        probs = jnp.exp(scores - lse_part)
        rounded = probs.astype(bf16)
        d_v = jnp.einsum("hqk,qhe->khe", rounded, do_part, preferred_element_type=f32)
        d_probs = jnp.einsum("qhe,khe->hqk", do_part, v_part, preferred_element_type=f32)
        inner = jnp.sum(d_probs * probs, axis=-1, keepdims=True)
        d_scores = (probs * (d_probs - inner)).astype(bf16)
        d_q = jnp.einsum("hqk,khe->qhe", d_scores, k_part, preferred_element_type=f32)
        d_k = jnp.einsum("hqk,qhe->khe", d_scores, q_part, preferred_element_type=f32)
        d_q = d_q * HEAD ** (-0.5)
        d_k = d_k * HEAD ** (-0.5)
        return (d_q.astype(bf16), d_k.astype(bf16), d_v.astype(bf16))

    d_qs, d_ks, d_vs = lax.map(
        attend_back,
        (
            split_heads(query),
            split_heads(keys),
            split_heads(values),
            logsum,
            split_heads(d_attended),
        ),
    )
    return (join_heads(d_qs), join_heads(d_ks), join_heads(d_vs))


class Links:

    def __init__(self):
        self.count = lax.axis_size("narrow")
        self.wide = lax.axis_size("wide")
        self.x = lax.axis_index("narrow")
        spot = lax.axis_index("wide")
        self.core = spot % 2
        self.y = spot // 2 % 2
        self.z = spot // 4
        self.depth = self.wide // 4
        self.direct = self.count == 2 and self.wide == 16

    def table(self, move):
        pairs = []
        for i in range(self.count * self.wide):
            x = i % self.count
            spot = i // self.count
            to = move(x, spot // 2 % 2, spot // 4, spot % 2)
            if to is not None:
                pairs.append((i, ((to[2] * 2 + to[1]) * 2 + to[3]) * self.count + to[0]))
        return pairs

    def send(self, value, move):
        return lax.ppermute(value, AXES, self.table(move))

    def over_x(self, value):
        return self.send(value, lambda x, y, z, c: (1 - x, y, z, c))

    def over_y(self, value):
        return self.send(value, lambda x, y, z, c: (x, 1 - y, z, c))

    def over_core(self, value):
        return self.send(value, lambda x, y, z, c: (x, y, z, 1 - c))


def pick(which, zero, one):
    return jnp.where(which == 0, zero, one)


def gather_other(links, shard):
    rows, columns = shard.shape
    tiles = rows // 8
    span = -(-tiles // 4)
    starts = [tiles * k // 4 for k in range(4)]
    view = shard.reshape(tiles, 8, columns)
    start_of = jnp.array(starts, jnp.int32)
    mine = links.y * 2 + links.core

    def at(y, core):
        return start_of[y * 2 + core]

    piece = lax.dynamic_slice_in_dim(view, start_of[mine], span, 0)
    first = links.over_x(piece)
    second = links.over_y(first)
    third = links.over_core(first)
    fourth = links.over_core(second)
    whole = jnp.zeros((tiles, 8, columns), shard.dtype)
    y, core = (links.y, links.core)
    for value, spot in (
        (first, at(y, core)),
        (second, at(1 - y, core)),
        (third, at(y, 1 - core)),
        (fourth, at(1 - y, 1 - core)),
    ):
        whole = lax.dynamic_update_slice_in_dim(whole, value, spot, 0)
    return whole.reshape(rows, columns)


class Weight:

    def __init__(self, links, shard):
        self.links = links
        self.own = shard
        if links.direct:
            self.other = gather_other(links, shard)
        else:
            self.full = lax.all_gather(shard, "narrow", axis=0, tiled=True)

    def apply(self, left):
        if not self.links.direct:
            return dot(left, self.full)
        x = self.links.x
        half = left.shape[1] // 2
        mine = pick(x, left[:, :half], left[:, half:])
        theirs = pick(x, left[:, half:], left[:, :half])
        return dot(mine, self.own) + dot(theirs, self.other)

    def apply_t(self, left):
        if not self.links.direct:
            return dot_t(left, self.full)
        x = self.links.x
        mine = dot_t(left, self.own)
        theirs = dot_t(left, self.other)
        return jnp.concatenate([pick(x, mine, theirs), pick(x, theirs, mine)], axis=1)


def weight_grad(links, left, right):
    if not links.direct:
        grad = tdot(left, right).astype(bf16)
        grad = lax.psum_scatter(grad, "narrow", scatter_dimension=0, tiled=True)
        return lax.psum_scatter(grad, "wide", scatter_dimension=1, tiled=True).astype(f32)
    x, y, z, core = (links.x, links.y, links.z, links.core)
    rows, columns = (left.shape[1], right.shape[1])
    half = rows // 2
    unit = columns // 8
    right_own = pick(core, right[:, : columns // 2], right[:, columns // 2 :])
    right_away = pick(core, right[:, columns // 2 :], right[:, : columns // 2])
    right_all = jnp.concatenate([right_own, links.over_core(right_away)], axis=0)
    left_all = jnp.concatenate([left, links.over_core(left)], axis=0)
    left_own = pick(x, left_all[:, :half], left_all[:, half:])
    left_away = pick(x, left_all[:, half:], left_all[:, :half])
    cut = [right_all[:, k * unit : (k + 1) * unit] for k in range(4)]
    near = [pick(y, cut[0], cut[1]), pick(y, cut[2], cut[3])]
    far = [pick(y, cut[1], cut[0]), pick(y, cut[3], cut[2])]

    def both(one, two):
        return jnp.stack([one.astype(bf16), two.astype(bf16)])

    got_x = links.over_x(both(tdot(far[0], left_away), tdot(near[0], left_away)))
    got_y = links.over_y(both(tdot(far[1], left_away), tdot(far[1], left_own)))
    sum_far = tdot(far[0], left_own) + got_x[0].astype(f32)
    even = tdot(near[0], left_own) + got_x[1].astype(f32)
    sum_away = tdot(near[1], left_away) + got_y[0].astype(f32)
    odd = tdot(near[1], left_own) + got_y[1].astype(f32)
    even = even + links.over_y(sum_far.astype(bf16)).astype(f32)
    odd = odd + links.over_x(sum_away.astype(bf16)).astype(f32)
    low = z % 2 == 0
    even_b, odd_b = (even.astype(bf16), odd.astype(bf16))
    same = jnp.where(low, odd_b, even_b)
    straight = jnp.where(low, even_b, odd_b)
    got_1 = links.send(same, lambda x, y, z, c: (x, y, z ^ 1, c) if z // 2 == c else None)
    got_2 = links.send(straight, lambda x, y, z, c: (x, y, z ^ 2, c) if z // 2 != c else None)
    got_3 = links.send(same, lambda x, y, z, c: (x, y, z ^ 3, c) if z // 2 != c else None)
    total = jnp.where(low, even, odd)
    total = total + got_1.astype(f32) + got_2.astype(f32) + got_3.astype(f32)
    part = unit // 2
    zero_part, one_part = (total[:part], total[part:])
    got = links.send(
        pick(core, one_part, zero_part),
        lambda x, y, z, c: (x, y, z, 1 - c) if z // 2 == c else None,
    )
    result = jnp.where(z // 2 == core, pick(core, zero_part, one_part), got)
    return result.T


def gather_vectors(links, vectors):
    lengths = [v.shape[0] for v in vectors]
    if not links.direct:
        return [lax.all_gather(v, "narrow", axis=0, tiled=True).astype(f32) for v in vectors]
    packed = jnp.concatenate(vectors)
    other = links.over_x(packed)
    full = []
    at = 0
    for length in lengths:
        mine, theirs = (packed[at : at + length], other[at : at + length])
        joined = jnp.concatenate([pick(links.x, mine, theirs), pick(links.x, theirs, mine)])
        full.append(joined.astype(f32))
        at += length
    return full


def vector_grads(links, sums):
    lengths = [v.shape[0] for v in sums]
    total = lax.psum(jnp.concatenate(sums), AXES)
    parts = []
    at = 0
    for length in lengths:
        own = length // links.count
        parts.append(lax.dynamic_slice_in_dim(total, at + links.x * own, own, 0))
        at += length
    return parts


def local(
    tokens,
    lengths,
    dropped,
    cotangent,
    first_gain,
    first_shift,
    qkv_weight,
    query_bias,
    value_bias,
    out_weight,
    out_bias,
    second_gain,
    second_shift,
    up_weight,
    up_bias,
    down_weight,
    down_bias,
):
    links = Links()
    rows, width = tokens.shape[1:]
    mask = key_mask(lengths[0], dropped[0], rows)
    inputs = tokens[0].astype(f32)
    grad_out = cotangent[0]
    gain1, shift1, q_bias, v_bias, o_bias, gain2, shift2, d_bias, u_bias = gather_vectors(
        links,
        [
            first_gain,
            first_shift,
            query_bias,
            value_bias,
            out_bias,
            second_gain,
            second_shift,
            down_bias,
            up_bias,
        ],
    )
    w_qkv = Weight(links, qkv_weight)
    w_out = Weight(links, out_weight)
    w_up = Weight(links, up_weight)
    w_down = Weight(links, down_weight)
    first = normed(inputs, gain1, shift1).astype(bf16)
    mixed = w_qkv.apply(first)
    query = (mixed[:, :width] + q_bias).astype(bf16)
    keys = mixed[:, width : 2 * width].astype(bf16)
    values = (mixed[:, 2 * width :] + v_bias).astype(bf16)
    attended, logsum = attention(query, keys, values, mask)
    middle = inputs + (w_out.apply(attended) + o_bias)
    second = normed(middle, gain2, shift2).astype(bf16)
    hidden = w_up.apply(second) + u_bias
    active = jax.nn.gelu(hidden, approximate=True).astype(bf16)
    g_down = weight_grad(links, active, grad_out)
    result = middle + (w_down.apply(active) + d_bias)
    output = result.astype(bf16)[None]
    d_active = w_down.apply_t(grad_out)
    unused, gelu_pull = jax.vjp(lambda v: jax.nn.gelu(v, approximate=True), hidden)
    d_hidden = gelu_pull(d_active)[0].astype(bf16)
    g_up = weight_grad(links, second, d_hidden)
    d_second = w_up.apply_t(d_hidden)
    unused, norm_pull = jax.vjp(normed, middle, gain2, shift2)
    d_middle, d_gain2, d_shift2 = norm_pull(d_second)
    d_middle = d_middle + grad_out.astype(f32)
    d_branch = d_middle.astype(bf16)
    g_out = weight_grad(links, attended, d_branch)
    d_attended = w_out.apply_t(d_branch).astype(bf16)
    d_query, d_keys, d_values = attention_back(query, keys, values, logsum, d_attended, mask)
    d_mixed = jnp.concatenate([d_query, d_keys, d_values], axis=1)
    g_qkv = weight_grad(links, first, d_mixed)
    d_first = w_qkv.apply_t(d_mixed)
    unused, first_pull = jax.vjp(normed, inputs, gain1, shift1)
    d_inputs, d_gain1, d_shift1 = first_pull(d_first)
    grad_tokens = (d_middle + d_inputs)[None]

    def column_sum(values):
        return jnp.sum(values.astype(f32), axis=0)

    v_gain1, v_shift1, v_q, v_v, v_o, v_gain2, v_shift2, v_up, v_down = vector_grads(
        links,
        [
            d_gain1,
            d_shift1,
            column_sum(d_query),
            column_sum(d_values),
            column_sum(d_branch),
            d_gain2,
            d_shift2,
            column_sum(d_hidden),
            column_sum(grad_out),
        ],
    )
    return (
        output,
        grad_tokens,
        v_gain1,
        v_shift1,
        g_qkv,
        v_q,
        v_v,
        g_out,
        v_o,
        v_gain2,
        v_shift2,
        g_up,
        v_up,
        g_down,
        v_down,
    )


def solution(mesh):
    batch = P(AXES, None, None)
    vector = P("narrow")
    matrix = P("narrow", None)
    return jax.shard_map(
        local,
        mesh=mesh,
        in_specs=(
            batch,
            P(AXES),
            P(AXES),
            batch,
            vector,
            vector,
            matrix,
            vector,
            vector,
            matrix,
            vector,
            vector,
            vector,
            matrix,
            vector,
            matrix,
            vector,
        ),
        out_specs=(
            batch,
            batch,
            vector,
            vector,
            P("narrow", "wide"),
            vector,
            vector,
            P("narrow", "wide"),
            vector,
            vector,
            vector,
            P("narrow", "wide"),
            vector,
            P("narrow", "wide"),
            vector,
        ),
        check_vma=False,
    )
```

profile of v0, /device:TPU:0, one launch (start us, length us, event | category | flops | bytes accessed | tf_op | source)
XLA Modules:
  0.0 569.3 jit_solution(4175647565305170686)
XLA Ops:
  4.1 2.5 constant_dynamic-slice_fusion.1
  6.6 3.0 collective-permute-start.9
  10.4 2.3 constant_dynamic-slice_fusion.3
  12.7 2.0 collective-permute-start.1
  16.8 5.7 fusion.200
  22.5 2.5 constant_dynamic-slice_fusion
  30.9 35.9 %collective-permute-done = bf16[6720]{0:T(1024)(128)(2,1)S(1)} collective-permute-done((bf16[6720]{0:T(1024)(128)(2,1)S(1)}, bf16[6720]{0:T(1024)(128)(2,1)S(1)}, u32[]{:S(2)}, u32[]{:S(2)}) %collective-permute-start) | collective-permute-done | bytes 13472 | tf_op jit(solution)/shard_map/ppermute | solution.py:125
  67.5 4.1 fusion.169
  79.7 6.2 %collective-permute-done.6 = bf16[18,8,1120]{2,1,0:T(8,128)(2,1)S(1)} collective-permute-done((bf16[18,8,1120]{2,1,0:T(8,128)(2,1)}, bf16[18,8,1120]{2,1,0:T(8,128)(2,1)S(1)}, u32[]{:S(2)}, u32[]{:S(2)}) %collective-permute-start.6) | collective-permute-done | bytes 322592 | tf_op jit(solution)/shard_map/ppermute | solution.py:125
  89.5 14.6 %collective-permute-done.13 = bf16[70,8,1120]{2,1,0:T(8,128)(2,1)S(1)} collective-permute-done((bf16[70,8,1120]{2,1,0:T(8,128)(2,1)S(1)}, bf16[70,8,1120]{2,1,0:T(8,128)(2,1)S(1)}, u32[]{:S(2)}, u32[]{:S(2)}) %collective-permute-start.13) | collective-permute-done | bytes 1254432 | tf_op jit(solution)/shard_map/ppermute | solution.py:125
  108.6 2.6 collective-permute-done.2
  112.0 26.9 %collective-permute-done.14 = bf16[70,8,1120]{2,1,0:T(8,128)(2,1)} collective-permute-done((bf16[70,8,1120]{2,1,0:T(8,128)(2,1)S(1)}, bf16[70,8,1120]{2,1,0:T(8,128)(2,1)}, u32[]{:S(2)}, u32[]{:S(2)}) %collective-permute-start.14) | collective-permute-done | bytes 1254432 | tf_op jit(solution)/shard_map/ppermute | solution.py:125
  140.7 25.5 %collective-permute-done.10 = bf16[18,8,4480]{2,1,0:T(8,128)(2,1)} collective-permute-done((bf16[18,8,4480]{2,1,0:T(8,128)(2,1)}, bf16[18,8,4480]{2,1,0:T(8,128)(2,1)}, u32[]{:S(2)}, u32[]{:S(2)}) %collective-permute-start.10) | collective-permute-done | bytes 1290272 | tf_op jit(solution)/shard_map/ppermute | solution.py:125
  167.7 2.3 copy-done.24
  170.1 2.0 convolution_add_fusion.1
  174.6 10.6 %while.28 = (s32[]{:T(128)}, bf16[4,256,5,56]{1,3,2,0:T(8,128)(2,1)}, f32[4,5,256,1]{2,1,3,0:T(8,128)S(1)}, bf16[4,256,5,56]{1,3,2,0:T(8,128)(2,1)}, bf16[4,256,...) while((s32[]{:T(128)}, ...), condition=%wide.region_5.6_spmd.clone, body=%wide.region_2.5_spmd.clone.sunk | while | flops 76354304 | bytes 4689241 | solution.py:65
  175.4 1.9 fusion.284
  178.0 1.9 fusion.284
  180.7 1.9 fusion.284
  183.3 1.9 fusion.284
  186.3 1.9 fusion.166
  188.3 2.4 fusion.213
  191.8 2.7 constant_dynamic-update-slice_fusion.5
  194.5 2.0 fusion.163
  197.8 2.5 broadcast_select_fusion.18
  202.1 1.8 broadcast_select_fusion.5
  205.9 7.2 %convert_reduce_fusion = (f32[4480]{0:T(1024)S(1)}, bf16[256,4480]{1,0:T(8,128)(2,1)S(1)}, bf16[256,4480]{1,0:T(8,128)(2,1)}) fusion(f32[256,2240]{1,0:T(8,128)S(1)} %get-tuple-element.203, f32[256,2240]{1,0:T(8,128)S(1)} %get-tuple-element.202, f32[4480]{0:T(1024)S(1)} %copy-done.35, f32[256,4480]{1,0:T(8,128)S(1)} %fusion.163, ...), kind=kOutput, calls=%fused_computation.88 | convolution fusion | flops 1315610240 | bytes 19389440 | tf_op jit(solution)/shard_map/dot_general | solution.py:15
  213.1 1.8 broadcast_select_fusion.2
  225.7 22.3 %while.29 = (s32[]{:T(128)}, bf16[4,256,5,56]{1,3,2,0:T(8,128)(2,1)}, bf16[4,256,5,56]{1,3,2,0:T(8,128)(2,1)}, bf16[4,256,5,56]{1,3,2,0:T(8,128)(2,1)}, bf16[4,2...) while((s32[]{:T(128)}, ...), condition=%wide.region_12.13_spmd.clone, body=%wide.region_10.12_spmd.clone.sunk | while | flops 187069184 | bytes 13723021 | solution.py:88
  248.0 3.0 broadcast_select_fusion.6
  251.0 4.4 fusion.150
  255.8 6.7 %fusion.128 = f32[256,1120]{0,1:T(8,128)} fusion(bf16[2240,1120]{1,0:T(8,128)(2,1)} %param.40, pred[]{:T(512)S(6)} %eq.19, bf16[256,4480]{1,0:T(8,128)(2,1)} %get-tuple-element.206), kind=kOutput, calls=%fused_computation.196 | convolution fusion | flops 1285079040 | bytes 8667137 | tf_op jit(solution)/shard_map/dot_general | solution.py:15
  262.5 2.6 copy.63
  265.8 4.1 broadcast_select_fusion.33
  272.9 5.0 fusion.95
  280.9 40.1 %psum.7 = f32[13440]{0:T(1024)S(1)} all-reduce(f32[13440]{0:T(1024)S(1)} %concatenate.137), channel_id=1, replica_groups=mesh['wide'=16,'narrow'=2] {'wide','narrow'}, use_global_device_ids=true, to_apply=%region_24.25 | all-reduce | flops 13440 | bytes 107520 | tf_op jit(solution)/shard_map/psum | solution.py:265
  323.6 2.3 collective-permute-start.31
  328.9 4.7 collective-permute-done.31
  334.0 1.8 collective-permute-start.32
  337.3 2.6 collective-permute-done.32
  340.2 2.6 collective-permute-done.30
  343.2 3.4 collective-permute-start.33
  354.1 1.9 copy.57
  356.1 1.8 copy.60
  361.8 2.4 copy.64
  364.2 2.7 fusion.151
  368.7 2.0 collective-permute-start.39
  371.5 11.1 %collective-permute-done.21 = bf16[2,420,560]{2,0,1:T(2,128)(2,1)} collective-permute-done((bf16[2,420,560]{2,0,1:T(2,128)(2,1)}, bf16[2,420,560]{2,0,1:T(2,128)(2,1)}, u32[]{:S(2)}, u32[]{:S(2)}) %collective-permute-start.21) | collective-permute-done | bytes 940832 | tf_op jit(solution)/shard_map/ppermute | solution.py:125
  382.6 3.3 fusion.209
  388.2 3.5 fusion.210
  395.5 29.3 %collective-permute-done.22 = bf16[420,560]{1,0:T(8,128)(2,1)S(1)} collective-permute-done((bf16[420,560]{1,0:T(8,128)(2,1)S(1)}, bf16[420,560]{1,0:T(8,128)(2,1)S(1)}, u32[]{:S(2)}, u32[]{:S(2)}) %collective-permute-start.22) | collective-permute-done | bytes 470432 | tf_op jit(solution)/shard_map/ppermute | solution.py:125
  425.9 2.5 collective-permute-start.23
  431.2 4.6 broadcast_select_fusion
  445.5 12.5 %collective-permute-done.24 = bf16[420,560]{1,0:T(8,128)(2,1)S(1)} collective-permute-done((bf16[420,560]{1,0:T(8,128)(2,1)S(1)}, bf16[420,560]{1,0:T(8,128)(2,1)S(1)}, u32[]{:S(2)}, u32[]{:S(2)}) %collective-permute-start.24) | collective-permute-done | bytes 470432 | tf_op jit(solution)/shard_map/ppermute | solution.py:125
  461.4 10.1 %collective-permute-done.51 = bf16[2,140,2240]{2,0,1:T(2,128)(2,1)S(1)} collective-permute-done((bf16[2,140,2240]{2,0,1:T(2,128)(2,1)S(1)}, bf16[2,140,2240]{2,0,1:T(2,128)(2,1)S(1)}, u32[]{:S(2)}, u32[]{:S(2)}) %collective-permute-start.51) | collective-permute-done | bytes 1254432 | tf_op jit(solution)/shard_map/ppermute | solution.py:125
  471.4 1.8 fusion.207
  474.1 15.1 %collective-permute-done.49 = bf16[2,140,2240]{2,0,1:T(2,128)(2,1)S(1)} collective-permute-done((bf16[2,140,2240]{2,0,1:T(2,128)(2,1)S(1)}, bf16[2,140,2240]{2,0,1:T(2,128)(2,1)S(1)}, u32[]{:S(2)}, u32[]{:S(2)}) %collective-permute-start.49) | collective-permute-done | bytes 1254432 | tf_op jit(solution)/shard_map/ppermute | solution.py:125
  489.2 1.8 fusion.208
  493.1 1.9 collective-permute-start.43
  499.5 2.8 collective-permute-done.50
  504.3 9.6 %collective-permute-done.43 = bf16[560,560]{1,0:T(8,128)(2,1)S(1)} collective-permute-done((bf16[560,560]{1,0:T(8,128)(2,1)S(1)}, bf16[560,560]{1,0:T(8,128)(2,1)S(1)}, u32[]{:S(2)}, u32[]{:S(2)}) %collective-permute-start.43) | collective-permute-done | bytes 627232 | tf_op jit(solution)/shard_map/ppermute | solution.py:125
  513.9 1.9 collective-permute-start.53
  515.8 16.9 %collective-permute-done.44 = bf16[560,560]{1,0:T(8,128)(2,1)S(1)} collective-permute-done((bf16[560,560]{1,0:T(8,128)(2,1)S(1)}, bf16[560,560]{1,0:T(8,128)(2,1)S(1)}, u32[]{:S(2)}, u32[]{:S(2)}) %collective-permute-start.44) | collective-permute-done | bytes 627232 | tf_op jit(solution)/shard_map/ppermute | solution.py:125
  537.2 26.2 %collective-permute-done.54 = bf16[140,2240]{1,0:T(8,128)(2,1)S(1)} collective-permute-done((bf16[140,2240]{1,0:T(8,128)(2,1)S(1)}, bf16[140,2240]{1,0:T(8,128)(2,1)S(1)}, u32[]{:S(2)}, u32[]{:S(2)}) %collective-permute-start.54) | collective-permute-done | bytes 627232 | tf_op jit(solution)/shard_map/ppermute | solution.py:125
  (396 shorter events, 140.3 us)
Async XLA Ops:
  6.6 99.9 %collective-permute-start.9 = (bf16[18,8,4480]{2,1,0:T(8,128)(2,1)}, bf16[18,8,4480]{2,1,0:T(8,128)(2,1)}, u32[]{:S(2)}, u32[]{:S(2)}) collective-permute-start(bf16[18,8,4480]{2,1,0:T(8,128)(2,1)} %constant_dynamic-slice_fusion.1), channel_id=1, source_target_pairs={{0,1},{1,0},{2,3},{3,2},{4,5},{5,4},{6,7},{7,6},{8,9},{9,8},{10,11... | collective-permute-start | bytes 3870728 | tf_op jit(solution)/shard_map/ppermute | solution.py:125
  10.4 65.4 %collective-permute-start.5 = (bf16[18,8,1120]{2,1,0:T(8,128)(2,1)}, bf16[18,8,1120]{2,1,0:T(8,128)(2,1)}, u32[]{:S(2)}, u32[]{:S(2)}) collective-permute-start(bf16[18,8,1120]{2,1,0:T(8,128)(2,1)} %constant_dynamic-slice_fusion.2), channel_id=1, source_target_pairs={{0,1},{1,0},{2,3},{3,2},{4,5},{5,4},{6,7},{7,6},{8,9},{9,8},{10,11... | collective-permute-start | bytes 967688 | tf_op jit(solution)/shard_map/ppermute | solution.py:125
  12.7 73.3 %collective-permute-start.1 = (bf16[18,8,3360]{2,1,0:T(8,128)(2,1)}, bf16[18,8,3360]{2,1,0:T(8,128)(2,1)}, u32[]{:S(2)}, u32[]{:S(2)}) collective-permute-start(bf16[18,8,3360]{2,1,0:T(8,128)(2,1)} %constant_dynamic-slice_fusion.3), channel_id=1, source_target_pairs={{0,1},{1,0},{2,3},{3,2},{4,5},{5,4},{6,7},{7,6},{8,9},{9,8},{10,11... | collective-permute-start | bytes 2903048 | tf_op jit(solution)/shard_map/ppermute | solution.py:125
  14.9 52.0 %collective-permute-start = (bf16[6720]{0:T(1024)(128)(2,1)S(1)}, bf16[6720]{0:T(1024)(128)(2,1)S(1)}, u32[]{:S(2)}, u32[]{:S(2)}) collective-permute-start(bf16[6720]{0:T(1024)(128)(2,1)S(1)} %concatenate.120), channel_id=1, source_target_pairs={{0,1},{1,0},{2,3},{3,2},{4,5},{5,4},{6,7},{7,6},{8,9},{9,8},{10,11... | collective-permute-start | bytes 40328 | tf_op jit(solution)/shard_map/ppermute | solution.py:125
  15.0 58.3 %collective-permute-start.47 = (bf16[256,560]{0,1:T(8,128)(2,1)S(1)}, bf16[256,560]{0,1:T(8,128)(2,1)S(1)}, u32[]{:S(2)}, u32[]{:S(2)}) collective-permute-start(bf16[256,560]{0,1:T(8,128)(2,1)S(1)} %get-tuple-element.251), channel_id=1, source_target_pairs={{0,2},{1,3},{2,0},{3,1},{4,6},{5,7},{6,4},{7,5},{8,10},{9,11},{10,... | collective-permute-start | bytes 860168 | tf_op jit(solution)/shard_map/ppermute | solution.py:125
  15.5 51.6 %copy-start.36 = (f32[256]{0:T(256)}, f32[256]{0:T(256)S(1)}, u32[]{:S(2)}) copy-start(f32[256]{0:T(256)S(1)} %fusion.195) | copy-start | bytes 3076
  71.7 6.8 %collective-permute-start.18 = (bf16[256,1120]{0,1:T(8,128)(2,1)S(1)}, bf16[256,1120]{0,1:T(8,128)(2,1)S(1)}, u32[]{:S(2)}, u32[]{:S(2)}) collective-permute-start(bf16[256,1120]{0,1:T(8,128)(2,1)S(1)} %fusion.139), channel_id=1, source_target_pairs={{0,2},{1,3},{2,0},{3,1},{4,6},{5,7},{6,4},{7,5},{8,10},{9,11},{10,... | collective-permute-start | bytes 1720328 | tf_op jit(solution)/shard_map/ppermute | solution.py:125
  73.3 30.7 %collective-permute-start.13 = (bf16[70,8,1120]{2,1,0:T(8,128)(2,1)S(1)}, bf16[70,8,1120]{2,1,0:T(8,128)(2,1)S(1)}, u32[]{:S(2)}, u32[]{:S(2)}) collective-permute-start(bf16[70,8,1120]{2,1,0:T(8,128)(2,1)S(1)} %copy-done.30), channel_id=1, source_target_pairs={{0,1},{1,0},{2,3},{3,2},{4,5},{5,4},{6,7},{7,6},{8,9},{9,8},{10,11... | collective-permute-start | bytes 3763208 | tf_op jit(solution)/shard_map/ppermute | solution.py:125
  75.8 10.1 %collective-permute-start.6 = (bf16[18,8,1120]{2,1,0:T(8,128)(2,1)}, bf16[18,8,1120]{2,1,0:T(8,128)(2,1)S(1)}, u32[]{:S(2)}, u32[]{:S(2)}) collective-permute-start(bf16[18,8,1120]{2,1,0:T(8,128)(2,1)} %collective-permute-done.5), channel_id=1, source_target_pairs={{0,4},{1,5},{2,6},{3,7},{4,0},{5,1},{6,2},{7,3},{8,12},{9,13},{10,... | collective-permute-start | bytes 967688 | tf_op jit(solution)/shard_map/ppermute | solution.py:125
  78.5 7.5 %collective-permute-start.7 = (bf16[18,8,1120]{2,1,0:T(8,128)(2,1)}, bf16[18,8,1120]{2,1,0:T(8,128)(2,1)S(1)}, u32[]{:S(2)}, u32[]{:S(2)}) collective-permute-start(bf16[18,8,1120]{2,1,0:T(8,128)(2,1)} %collective-permute-done.5), channel_id=1, source_target_pairs={{0,2},{1,3},{2,0},{3,1},{4,6},{5,7},{6,4},{7,5},{8,10},{9,11},{10,... | collective-permute-start | bytes 967688 | tf_op jit(solution)/shard_map/ppermute | solution.py:125
  85.9 3.5 collective-permute-start.8
  86.0 25.2 %collective-permute-start.2 = (bf16[18,8,3360]{2,1,0:T(8,128)(2,1)}, bf16[18,8,3360]{2,1,0:T(8,128)(2,1)S(1)}, u32[]{:S(2)}, u32[]{:S(2)}) collective-permute-start(bf16[18,8,3360]{2,1,0:T(8,128)(2,1)} %collective-permute-done.1), channel_id=1, source_target_pairs={{0,4},{1,5},{2,6},{3,7},{4,0},{5,1},{6,2},{7,3},{8,12},{9,13},{10,... | collective-permute-start | bytes 2903048 | tf_op jit(solution)/shard_map/ppermute | solution.py:125
  87.6 23.7 %collective-permute-start.3 = (bf16[18,8,3360]{2,1,0:T(8,128)(2,1)}, bf16[18,8,3360]{2,1,0:T(8,128)(2,1)S(1)}, u32[]{:S(2)}, u32[]{:S(2)}) collective-permute-start(bf16[18,8,3360]{2,1,0:T(8,128)(2,1)} %collective-permute-done.1), channel_id=1, source_target_pairs={{0,2},{1,3},{2,0},{3,1},{4,6},{5,7},{6,4},{7,5},{8,10},{9,11},{10,... | collective-permute-start | bytes 2903048 | tf_op jit(solution)/shard_map/ppermute | solution.py:125
  89.5 16.3 %copy-start.22 = (bf16[70,8,1120]{2,1,0:T(8,128)(2,1)}, bf16[70,8,1120]{2,1,0:T(8,128)(2,1)S(1)}, u32[]{:S(2)}) copy-start(bf16[70,8,1120]{2,1,0:T(8,128)(2,1)S(1)} %constant_dynamic-update-slice_fusion.8) | copy-start | bytes 3763204
  104.1 34.9 %collective-permute-start.14 = (bf16[70,8,1120]{2,1,0:T(8,128)(2,1)S(1)}, bf16[70,8,1120]{2,1,0:T(8,128)(2,1)}, u32[]{:S(2)}, u32[]{:S(2)}) collective-permute-start(bf16[70,8,1120]{2,1,0:T(8,128)(2,1)S(1)} %collective-permute-done.13), channel_id=1, source_target_pairs={{0,4},{1,5},{2,6},{3,7},{4,0},{5,1},{6,2},{7,3},{8,12},{9,13},{10,... | collective-permute-start | bytes 3763208 | tf_op jit(solution)/shard_map/ppermute | solution.py:125
  105.9 34.6 %collective-permute-start.15 = (bf16[70,8,1120]{2,1,0:T(8,128)(2,1)S(1)}, bf16[70,8,1120]{2,1,0:T(8,128)(2,1)S(1)}, u32[]{:S(2)}, u32[]{:S(2)}) collective-permute-start(bf16[70,8,1120]{2,1,0:T(8,128)(2,1)S(1)} %collective-permute-done.13), channel_id=1, source_target_pairs={{0,2},{1,3},{2,0},{3,1},{4,6},{5,7},{6,4},{7,5},{8,10},{9,11},{10,... | collective-permute-start | bytes 3763208 | tf_op jit(solution)/shard_map/ppermute | solution.py:125
  106.4 59.7 %collective-permute-start.10 = (bf16[18,8,4480]{2,1,0:T(8,128)(2,1)}, bf16[18,8,4480]{2,1,0:T(8,128)(2,1)}, u32[]{:S(2)}, u32[]{:S(2)}) collective-permute-start(bf16[18,8,4480]{2,1,0:T(8,128)(2,1)} %collective-permute-done.9), channel_id=1, source_target_pairs={{0,4},{1,5},{2,6},{3,7},{4,0},{5,1},{6,2},{7,3},{8,12},{9,13},{10,... | collective-permute-start | bytes 3870728 | tf_op jit(solution)/shard_map/ppermute | solution.py:125
  111.2 80.6 %collective-permute-start.11 = (bf16[18,8,4480]{2,1,0:T(8,128)(2,1)}, bf16[18,8,4480]{2,1,0:T(8,128)(2,1)}, u32[]{:S(2)}, u32[]{:S(2)}) collective-permute-start(bf16[18,8,4480]{2,1,0:T(8,128)(2,1)} %collective-permute-done.9), channel_id=1, source_target_pairs={{0,2},{1,3},{2,0},{3,1},{4,6},{5,7},{6,4},{7,5},{8,10},{9,11},{10,... | collective-permute-start | bytes 3870728 | tf_op jit(solution)/shard_map/ppermute | solution.py:125
  111.3 56.3 %collective-permute-start.4 = (bf16[18,8,3360]{2,1,0:T(8,128)(2,1)S(1)}, bf16[18,8,3360]{2,1,0:T(8,128)(2,1)S(1)}, u32[]{:S(2)}, u32[]{:S(2)}) collective-permute-start(bf16[18,8,3360]{2,1,0:T(8,128)(2,1)S(1)} %collective-permute-done.2), channel_id=1, source_target_pairs={{0,2},{1,3},{2,0},{3,1},{4,6},{5,7},{6,4},{7,5},{8,10},{9,11},{10,... | collective-permute-start | bytes 2903048 | tf_op jit(solution)/shard_map/ppermute | solution.py:125
  139.0 61.4 %collective-permute-start.16 = (bf16[70,8,1120]{2,1,0:T(8,128)(2,1)}, bf16[70,8,1120]{2,1,0:T(8,128)(2,1)}, u32[]{:S(2)}, u32[]{:S(2)}) collective-permute-start(bf16[70,8,1120]{2,1,0:T(8,128)(2,1)} %collective-permute-done.14), channel_id=1, source_target_pairs={{0,2},{1,3},{2,0},{3,1},{4,6},{5,7},{6,4},{7,5},{8,10},{9,11},{10,... | collective-permute-start | bytes 3763208 | tf_op jit(solution)/shard_map/ppermute | solution.py:125
  140.7 31.4 %copy-start.2 = (bf16[280,8,1120]{2,1,0:T(8,128)(2,1)}, bf16[280,8,1120]{2,1,0:T(8,128)(2,1)S(1)}, u32[]{:S(2)}) copy-start(bf16[280,8,1120]{2,1,0:T(8,128)(2,1)S(1)} %constant_dynamic-update-slice_fusion.1) | copy-start | bytes 15052804
  166.2 38.2 %collective-permute-start.12 = (bf16[18,8,4480]{2,1,0:T(8,128)(2,1)}, bf16[18,8,4480]{2,1,0:T(8,128)(2,1)}, u32[]{:S(2)}, u32[]{:S(2)}) collective-permute-start(bf16[18,8,4480]{2,1,0:T(8,128)(2,1)} %collective-permute-done.10), channel_id=1, source_target_pairs={{0,2},{1,3},{2,0},{3,1},{4,6},{5,7},{6,4},{7,5},{8,10},{9,11},{10,... | collective-permute-start | bytes 3870728 | tf_op jit(solution)/shard_map/ppermute | solution.py:125
  191.2 5.3 collective-permute-start.38
  194.5 3.3 collective-permute-start.28
  255.4 174.3 %collective-permute-start.48 = (bf16[256,4480]{1,0:T(8,128)(2,1)}, bf16[256,4480]{1,0:T(8,128)(2,1)}, u32[]{:S(2)}, u32[]{:S(2)}) collective-permute-start(bf16[256,4480]{1,0:T(8,128)(2,1)} %get-tuple-element.206), channel_id=1, source_target_pairs={{0,2},{1,3},{2,0},{3,1},{4,6},{5,7},{6,4},{7,5},{8,10},{9,11},{10,... | collective-permute-start | bytes 6881288 | tf_op jit(solution)/shard_map/ppermute | solution.py:125
  262.5 10.4 %slice-start.2 = ((s8[5160960]{0:T(1024)(128)(4,1)}), s8[966656]{0:T(1024)(128)(4,1)S(1)}, s32[]{:S(2)}) async-start(s8[5160960]{0:T(1024)(128)(4,1)} %bitcast.402), calls=%async_computation.2 | async-start | bytes 1933312
  265.2 96.6 %collective-permute-start.37 = (bf16[256,2240]{0,1:T(8,128)(2,1)}, bf16[256,2240]{0,1:T(8,128)(2,1)}, u32[]{:S(2)}, u32[]{:S(2)}) collective-permute-start(bf16[256,2240]{0,1:T(8,128)(2,1)} %copy.63), channel_id=1, source_target_pairs={{0,2},{1,3},{2,0},{3,1},{4,6},{5,7},{6,4},{7,5},{8,10},{9,11},{10,... | collective-permute-start | bytes 3440648 | tf_op jit(solution)/shard_map/ppermute | solution.py:125
  265.3 56.4 %collective-permute-start.27 = (bf16[256,560]{0,1:T(8,128)(2,1)}, bf16[256,560]{0,1:T(8,128)(2,1)}, u32[]{:S(2)}, u32[]{:S(2)}) collective-permute-start(bf16[256,560]{0,1:T(8,128)(2,1)} %get-tuple-element.257), channel_id=1, source_target_pairs={{0,2},{1,3},{2,0},{3,1},{4,6},{5,7},{6,4},{7,5},{8,10},{9,11},{10,... | collective-permute-start | bytes 860168 | tf_op jit(solution)/shard_map/ppermute | solution.py:125
  265.8 82.2 %collective-permute-start.17 = (bf16[256,1680]{0,1:T(8,128)(2,1)}, bf16[256,1680]{0,1:T(8,128)(2,1)}, u32[]{:S(2)}, u32[]{:S(2)}) collective-permute-start(bf16[256,1680]{0,1:T(8,128)(2,1)} %get-tuple-element.225), channel_id=1, source_target_pairs={{0,2},{1,3},{2,0},{3,1},{4,6},{5,7},{6,4},{7,5},{8,10},{9,11},{10,... | collective-permute-start | bytes 2580488 | tf_op jit(solution)/shard_map/ppermute | solution.py:125
  278.0 43.7 %copy-start.31 = (bf16[256,560]{0,1:T(8,128)(2,1)S(1)}, bf16[256,560]{0,1:T(8,128)(2,1)}, u32[]{:S(2)}) copy-start(bf16[256,560]{0,1:T(8,128)(2,1)} %get-tuple-element.258) | copy-start | bytes 860164
  278.0 44.8 %copy-start.7 = (bf16[512,560]{0,1:T(8,128)(2,1)S(1)}, bf16[512,560]{0,1:T(8,128)(2,1)}, u32[]{:S(2)}) copy-start(bf16[512,560]{0,1:T(8,128)(2,1)} %get-tuple-element.233) | copy-start | bytes 1720324
  280.7 42.4 %copy-start.6 = (bf16[512,560]{0,1:T(8,128)(2,1)S(1)}, bf16[512,560]{0,1:T(8,128)(2,1)}, u32[]{:S(2)}) copy-start(bf16[512,560]{0,1:T(8,128)(2,1)} %get-tuple-element.234) | copy-start | bytes 1720324
  323.6 10.0 %collective-permute-start.31 = (bf16[2,140,560]{2,1,0:T(8,128)(2,1)S(1)}, bf16[2,140,560]{2,1,0:T(8,128)(2,1)S(1)}, u32[]{:S(2)}, u32[]{:S(2)}) collective-permute-start(bf16[2,140,560]{2,1,0:T(8,128)(2,1)S(1)} %pad_maximum_fusion.21), channel_id=1, source_target_pairs={{0,4},{1,5},{2,6},{3,7},{4,0},{5,1},{6,2},{7,3},{8,12},{9,13},{10,... | collective-permute-start | bytes 940808 | tf_op jit(solution)/shard_map/ppermute | solution.py:125
  326.7 10.1 %collective-permute-start.29 = (bf16[2,140,560]{2,1,0:T(8,128)(2,1)S(1)}, bf16[2,140,560]{2,1,0:T(8,128)(2,1)S(1)}, u32[]{:S(2)}, u32[]{:S(2)}) collective-permute-start(bf16[2,140,560]{2,1,0:T(8,128)(2,1)S(1)} %pad_maximum_fusion.20), channel_id=1, source_target_pairs={{0,1},{1,0},{2,3},{3,2},{4,5},{5,4},{6,7},{7,6},{8,9},{9,8},{10,11... | collective-permute-start | bytes 940808 | tf_op jit(solution)/shard_map/ppermute | solution.py:125
  334.0 5.9 %collective-permute-start.32 = (bf16[140,560]{1,0:T(8,128)(2,1)S(1)}, bf16[140,560]{1,0:T(8,128)(2,1)S(1)}, u32[]{:S(2)}, u32[]{:S(2)}) collective-permute-start(bf16[140,560]{1,0:T(8,128)(2,1)S(1)} %fusion.133), channel_id=1, source_target_pairs={{0,1},{1,0},{2,3},{3,2},{4,5},{5,4},{6,7},{7,6},{8,9},{9,8},{10,11... | collective-permute-start | bytes 470408 | tf_op jit(solution)/shard_map/ppermute | solution.py:125
  337.2 5.6 collective-permute-start.30
  343.2 14.8 %collective-permute-start.33 = (bf16[140,560]{1,0:T(8,128)(2,1)S(1)}, bf16[140,560]{1,0:T(8,128)(2,1)S(1)}, u32[]{:S(2)}, u32[]{:S(2)}) collective-permute-start(bf16[140,560]{1,0:T(8,128)(2,1)S(1)} %get-tuple-element.246), channel_id=1, source_target_pairs={{0,8},{1,9},{4,12},{5,13},{8,0},{9,1},{12,4},{13,5},{18,26},{19,27... | collective-permute-start | bytes 470408 | tf_op jit(solution)/shard_map/ppermute | solution.py:125
  346.6 13.7 %collective-permute-start.35 = (bf16[140,560]{1,0:T(8,128)(2,1)S(1)}, bf16[140,560]{1,0:T(8,128)(2,1)S(1)}, u32[]{:S(2)}, u32[]{:S(2)}) collective-permute-start(bf16[140,560]{1,0:T(8,128)(2,1)S(1)} %get-tuple-element.246), channel_id=1, source_target_pairs={{2,26},{3,27},{6,30},{7,31},{10,18},{11,19},{14,22},{15,23},{16,8}... | collective-permute-start | bytes 470408 | tf_op jit(solution)/shard_map/ppermute | solution.py:125
  347.9 12.0 %collective-permute-start.34 = (bf16[140,560]{1,0:T(8,128)(2,1)S(1)}, bf16[140,560]{1,0:T(8,128)(2,1)S(1)}, u32[]{:S(2)}, u32[]{:S(2)}) collective-permute-start(bf16[140,560]{1,0:T(8,128)(2,1)S(1)} %get-tuple-element.245), channel_id=1, source_target_pairs={{2,18},{3,19},{6,22},{7,23},{10,26},{11,27},{14,30},{15,31},{16,0}... | collective-permute-start | bytes 470408 | tf_op jit(solution)/shard_map/ppermute | solution.py:125
  358.0 30.3 %collective-permute-start.19 = (bf16[2,420,560]{2,0,1:T(2,128)(2,1)}, bf16[2,420,560]{2,0,1:T(2,128)(2,1)}, u32[]{:S(2)}, u32[]{:S(2)}) collective-permute-start(bf16[2,420,560]{2,0,1:T(2,128)(2,1)} %copy.57), channel_id=1, source_target_pairs={{0,1},{1,0},{2,3},{3,2},{4,5},{5,4},{6,7},{7,6},{8,9},{9,8},{10,11... | collective-permute-start | bytes 2822408 | tf_op jit(solution)/shard_map/ppermute | solution.py:125
  359.9 22.7 %collective-permute-start.21 = (bf16[2,420,560]{2,0,1:T(2,128)(2,1)}, bf16[2,420,560]{2,0,1:T(2,128)(2,1)}, u32[]{:S(2)}, u32[]{:S(2)}) collective-permute-start(bf16[2,420,560]{2,0,1:T(2,128)(2,1)} %copy.60), channel_id=1, source_target_pairs={{0,4},{1,5},{2,6},{3,7},{4,0},{5,1},{6,2},{7,3},{8,12},{9,13},{10,... | collective-permute-start | bytes 2822408 | tf_op jit(solution)/shard_map/ppermute | solution.py:125
  368.7 72.9 %collective-permute-start.39 = (bf16[2,560,560]{2,1,0:T(8,128)(2,1)S(1)}, bf16[2,560,560]{2,1,0:T(8,128)(2,1)S(1)}, u32[]{:S(2)}, u32[]{:S(2)}) collective-permute-start(bf16[2,560,560]{2,1,0:T(8,128)(2,1)S(1)} %pad_maximum_fusion.3), channel_id=1, source_target_pairs={{0,1},{1,0},{2,3},{3,2},{4,5},{5,4},{6,7},{7,6},{8,9},{9,8},{10,11... | collective-permute-start | bytes 3763208 | tf_op jit(solution)/shard_map/ppermute | solution.py:125
  386.5 38.3 %collective-permute-start.22 = (bf16[420,560]{1,0:T(8,128)(2,1)S(1)}, bf16[420,560]{1,0:T(8,128)(2,1)S(1)}, u32[]{:S(2)}, u32[]{:S(2)}) collective-permute-start(bf16[420,560]{1,0:T(8,128)(2,1)S(1)} %fusion.111), channel_id=1, source_target_pairs={{0,1},{1,0},{2,3},{3,2},{4,5},{5,4},{6,7},{7,6},{8,9},{9,8},{10,11... | collective-permute-start | bytes 1411208 | tf_op jit(solution)/shard_map/ppermute | solution.py:125
  392.3 33.0 %collective-permute-start.20 = (bf16[420,560]{1,0:T(8,128)(2,1)S(1)}, bf16[420,560]{1,0:T(8,128)(2,1)S(1)}, u32[]{:S(2)}, u32[]{:S(2)}) collective-permute-start(bf16[420,560]{1,0:T(8,128)(2,1)S(1)} %fusion.110), channel_id=1, source_target_pairs={{0,4},{1,5},{2,6},{3,7},{4,0},{5,1},{6,2},{7,3},{8,12},{9,13},{10,... | collective-permute-start | bytes 1411208 | tf_op jit(solution)/shard_map/ppermute | solution.py:125
  394.0 46.2 %collective-permute-start.41 = (bf16[2,560,560]{2,1,0:T(8,128)(2,1)S(1)}, bf16[2,560,560]{2,1,0:T(8,128)(2,1)S(1)}, u32[]{:S(2)}, u32[]{:S(2)}) collective-permute-start(bf16[2,560,560]{2,1,0:T(8,128)(2,1)S(1)} %pad_maximum_fusion.4), channel_id=1, source_target_pairs={{0,4},{1,5},{2,6},{3,7},{4,0},{5,1},{6,2},{7,3},{8,12},{9,13},{10,... | collective-permute-start | bytes 3763208 | tf_op jit(solution)/shard_map/ppermute | solution.py:125
  425.9 18.0 %collective-permute-start.23 = (bf16[420,560]{1,0:T(8,128)(2,1)S(1)}, bf16[420,560]{1,0:T(8,128)(2,1)S(1)}, u32[]{:S(2)}, u32[]{:S(2)}) collective-permute-start(bf16[420,560]{1,0:T(8,128)(2,1)S(1)} %get-tuple-element.220), channel_id=1, source_target_pairs={{0,8},{1,9},{4,12},{5,13},{8,0},{9,1},{12,4},{13,5},{18,26},{19,27... | collective-permute-start | bytes 1411208 | tf_op jit(solution)/shard_map/ppermute | solution.py:125
  428.4 29.9 %collective-permute-start.25 = (bf16[420,560]{1,0:T(8,128)(2,1)S(1)}, bf16[420,560]{1,0:T(8,128)(2,1)S(1)}, u32[]{:S(2)}, u32[]{:S(2)}) collective-permute-start(bf16[420,560]{1,0:T(8,128)(2,1)S(1)} %get-tuple-element.220), channel_id=1, source_target_pairs={{2,26},{3,27},{6,30},{7,31},{10,18},{11,19},{14,22},{15,23},{16,8}... | collective-permute-start | bytes 1411208 | tf_op jit(solution)/shard_map/ppermute | solution.py:125
  429.7 28.3 %collective-permute-start.24 = (bf16[420,560]{1,0:T(8,128)(2,1)S(1)}, bf16[420,560]{1,0:T(8,128)(2,1)S(1)}, u32[]{:S(2)}, u32[]{:S(2)}) collective-permute-start(bf16[420,560]{1,0:T(8,128)(2,1)S(1)} %get-tuple-element.219), channel_id=1, source_target_pairs={{2,18},{3,19},{6,22},{7,23},{10,26},{11,27},{14,30},{15,31},{16,0}... | collective-permute-start | bytes 1411208 | tf_op jit(solution)/shard_map/ppermute | solution.py:125
  440.2 31.3 %collective-permute-start.51 = (bf16[2,140,2240]{2,0,1:T(2,128)(2,1)S(1)}, bf16[2,140,2240]{2,0,1:T(2,128)(2,1)S(1)}, u32[]{:S(2)}, u32[]{:S(2)}) collective-permute-start(bf16[2,140,2240]{2,0,1:T(2,128)(2,1)S(1)} %copy.68), channel_id=1, source_target_pairs={{0,4},{1,5},{2,6},{3,7},{4,0},{5,1},{6,2},{7,3},{8,12},{9,13},{10,... | collective-permute-start | bytes 3763208 | tf_op jit(solution)/shard_map/ppermute | solution.py:125
  441.6 19.0 %collective-permute-start.42 = (bf16[560,560]{1,0:T(8,128)(2,1)S(1)}, bf16[560,560]{1,0:T(8,128)(2,1)S(1)}, u32[]{:S(2)}, u32[]{:S(2)}) collective-permute-start(bf16[560,560]{1,0:T(8,128)(2,1)S(1)} %fusion.109), channel_id=1, source_target_pairs={{0,1},{1,0},{2,3},{3,2},{4,5},{5,4},{6,7},{7,6},{8,9},{9,8},{10,11... | collective-permute-start | bytes 1881608 | tf_op jit(solution)/shard_map/ppermute | solution.py:125
  444.0 121.4 %collective-permute-start.36 = (f32[70,560]{1,0:T(8,128)S(1)}, f32[70,560]{1,0:T(8,128)S(1)}, u32[]{:S(2)}, u32[]{:S(2)}) collective-permute-start(f32[70,560]{1,0:T(8,128)S(1)} %copy-done.33), channel_id=1, source_target_pairs={{0,2},{1,3},{4,6},{5,7},{8,10},{9,11},{12,14},{13,15},{18,16},{19,... | collective-permute-start | bytes 470408 | tf_op jit(solution)/shard_map/ppermute | solution.py:125
  458.0 31.2 %collective-permute-start.49 = (bf16[2,140,2240]{2,0,1:T(2,128)(2,1)S(1)}, bf16[2,140,2240]{2,0,1:T(2,128)(2,1)S(1)}, u32[]{:S(2)}, u32[]{:S(2)}) collective-permute-start(bf16[2,140,2240]{2,0,1:T(2,128)(2,1)S(1)} %copy.65), channel_id=1, source_target_pairs={{0,1},{1,0},{2,3},{3,2},{4,5},{5,4},{6,7},{7,6},{8,9},{9,8},{10,11... | collective-permute-start | bytes 3763208 | tf_op jit(solution)/shard_map/ppermute | solution.py:125
  458.3 33.9 %collective-permute-start.40 = (bf16[560,560]{1,0:T(8,128)(2,1)S(1)}, bf16[560,560]{1,0:T(8,128)(2,1)S(1)}, u32[]{:S(2)}, u32[]{:S(2)}) collective-permute-start(bf16[560,560]{1,0:T(8,128)(2,1)S(1)} %fusion.108), channel_id=1, source_target_pairs={{0,4},{1,5},{2,6},{3,7},{4,0},{5,1},{6,2},{7,3},{8,12},{9,13},{10,... | collective-permute-start | bytes 1881608 | tf_op jit(solution)/shard_map/ppermute | solution.py:125
  473.8 23.9 %collective-permute-start.52 = (bf16[140,2240]{1,0:T(8,128)(2,1)S(1)}, bf16[140,2240]{1,0:T(8,128)(2,1)S(1)}, u32[]{:S(2)}, u32[]{:S(2)}) collective-permute-start(bf16[140,2240]{1,0:T(8,128)(2,1)S(1)} %fusion.76), channel_id=1, source_target_pairs={{0,1},{1,0},{2,3},{3,2},{4,5},{5,4},{6,7},{7,6},{8,9},{9,8},{10,11... | collective-permute-start | bytes 1881608 | tf_op jit(solution)/shard_map/ppermute | solution.py:125
  491.6 10.7 %collective-permute-start.50 = (bf16[140,2240]{1,0:T(8,128)(2,1)S(1)}, bf16[140,2240]{1,0:T(8,128)(2,1)S(1)}, u32[]{:S(2)}, u32[]{:S(2)}) collective-permute-start(bf16[140,2240]{1,0:T(8,128)(2,1)S(1)} %fusion.75), channel_id=1, source_target_pairs={{0,4},{1,5},{2,6},{3,7},{4,0},{5,1},{6,2},{7,3},{8,12},{9,13},{10,... | collective-permute-start | bytes 1881608 | tf_op jit(solution)/shard_map/ppermute | solution.py:125
  493.1 20.8 %collective-permute-start.43 = (bf16[560,560]{1,0:T(8,128)(2,1)S(1)}, bf16[560,560]{1,0:T(8,128)(2,1)S(1)}, u32[]{:S(2)}, u32[]{:S(2)}) collective-permute-start(bf16[560,560]{1,0:T(8,128)(2,1)S(1)} %get-tuple-element.210), channel_id=1, source_target_pairs={{0,8},{1,9},{4,12},{5,13},{8,0},{9,1},{12,4},{13,5},{18,26},{19,27... | collective-permute-start | bytes 1881608 | tf_op jit(solution)/shard_map/ppermute | solution.py:125
  495.0 39.0 %collective-permute-start.45 = (bf16[560,560]{1,0:T(8,128)(2,1)S(1)}, bf16[560,560]{1,0:T(8,128)(2,1)S(1)}, u32[]{:S(2)}, u32[]{:S(2)}) collective-permute-start(bf16[560,560]{1,0:T(8,128)(2,1)S(1)} %get-tuple-element.210), channel_id=1, source_target_pairs={{2,26},{3,27},{6,30},{7,31},{10,18},{11,19},{14,22},{15,23},{16,8}... | collective-permute-start | bytes 1881608 | tf_op jit(solution)/shard_map/ppermute | solution.py:125
  497.6 35.1 %collective-permute-start.44 = (bf16[560,560]{1,0:T(8,128)(2,1)S(1)}, bf16[560,560]{1,0:T(8,128)(2,1)S(1)}, u32[]{:S(2)}, u32[]{:S(2)}) collective-permute-start(bf16[560,560]{1,0:T(8,128)(2,1)S(1)} %get-tuple-element.209), channel_id=1, source_target_pairs={{2,18},{3,19},{6,22},{7,23},{10,26},{11,27},{14,30},{15,31},{16,0}... | collective-permute-start | bytes 1881608 | tf_op jit(solution)/shard_map/ppermute | solution.py:125
  502.3 63.8 %collective-permute-start.26 = (f32[210,560]{1,0:T(8,128)S(1)}, f32[210,560]{1,0:T(8,128)S(1)}, u32[]{:S(2)}, u32[]{:S(2)}) collective-permute-start(f32[210,560]{1,0:T(8,128)S(1)} %slice_select_fusion.2), channel_id=1, source_target_pairs={{0,2},{1,3},{4,6},{5,7},{8,10},{9,11},{12,14},{13,15},{18,16},{19,... | collective-permute-start | bytes 1411208 | tf_op jit(solution)/shard_map/ppermute | solution.py:125
  513.9 22.0 %collective-permute-start.53 = (bf16[140,2240]{1,0:T(8,128)(2,1)S(1)}, bf16[140,2240]{1,0:T(8,128)(2,1)S(1)}, u32[]{:S(2)}, u32[]{:S(2)}) collective-permute-start(bf16[140,2240]{1,0:T(8,128)(2,1)S(1)} %get-tuple-element.212), channel_id=1, source_target_pairs={{0,8},{1,9},{4,12},{5,13},{8,0},{9,1},{12,4},{13,5},{18,26},{19,27... | collective-permute-start | bytes 1881608 | tf_op jit(solution)/shard_map/ppermute | solution.py:125
  532.7 30.7 %collective-permute-start.55 = (bf16[140,2240]{1,0:T(8,128)(2,1)S(1)}, bf16[140,2240]{1,0:T(8,128)(2,1)S(1)}, u32[]{:S(2)}, u32[]{:S(2)}) collective-permute-start(bf16[140,2240]{1,0:T(8,128)(2,1)S(1)} %get-tuple-element.212), channel_id=1, source_target_pairs={{2,26},{3,27},{6,30},{7,31},{10,18},{11,19},{14,22},{15,23},{16,8}... | collective-permute-start | bytes 1881608 | tf_op jit(solution)/shard_map/ppermute | solution.py:125
  534.0 29.4 %collective-permute-start.54 = (bf16[140,2240]{1,0:T(8,128)(2,1)S(1)}, bf16[140,2240]{1,0:T(8,128)(2,1)S(1)}, u32[]{:S(2)}, u32[]{:S(2)}) collective-permute-start(bf16[140,2240]{1,0:T(8,128)(2,1)S(1)} %get-tuple-element.211), channel_id=1, source_target_pairs={{2,18},{3,19},{6,22},{7,23},{10,26},{11,27},{14,30},{15,31},{16,0}... | collective-permute-start | bytes 1881608 | tf_op jit(solution)/shard_map/ppermute | solution.py:125
  535.9 31.2 %collective-permute-start.46 = (f32[280,560]{1,0:T(8,128)S(1)}, f32[280,560]{1,0:T(8,128)S(1)}, u32[]{:S(2)}, u32[]{:S(2)}) collective-permute-start(f32[280,560]{1,0:T(8,128)S(1)} %slice_select_fusion), channel_id=1, source_target_pairs={{0,2},{1,3},{4,6},{5,7},{8,10},{9,11},{12,14},{13,15},{18,16},{19,... | collective-permute-start | bytes 1881608 | tf_op jit(solution)/shard_map/ppermute | solution.py:125
  563.9 4.2 collective-permute-start.56
  (56 other events, 192.1 us)
where the time goes:
time: 580 us; the launch traced here: 569 us
  waiting for transfers between devices  260 us (45%)
  matrix products  97.7 us (17%)
  local copies, waits for them, and re-layouts  58.4 us (10%)
  starting transfers between devices  58.3 us (10%)
  other arithmetic  43.3 us (7%)
  blocking collectives  40.1 us (7%)
  between operations  11.6 us (2%)
    ppermute x57, waiting for transfers between devices, send(): return lax.ppermute(value, AXES, self.table(move))  260 us
    ppermute x57, starting transfers between devices, send(): return lax.ppermute(value, AXES, self.table(move))  58.3 us
    psum x1, blocking collectives, vector_grads(): total = lax.psum(jnp.concatenate(sums), AXES)  40.1 us
    dot_general x8, matrix products, dot(): return jnp.dot(left, right, preferred_element_type=f32)  31.4 us
    dot_general x8, matrix products, dot_t(): lax.dot_general(left, right, (((1,), (1,)), ((), ())), preferred_element_...  20.1 us
    dot_general x32, matrix products, tdot(): lax.dot_general(left, right, (((0,), (0,)), ((), ())), preferred_element_...  17.9 us
    select_n x15, other arithmetic, pick(): return jnp.where(which == 0, zero, one)  16.4 us
    dynamic_update_slice x16, local copies, waits for them, and re-layouts, gather_other(): whole = lax.dynamic_update_slice_in_dim(whole, value, spot, 0)  13.5 us
  transfers between devices with their start and end apart: 57, of which 22 were waited for; matrix products, arithmetic and copies ran while one was open for 24% of the time, Pallas kernels for 0%

commit v1 on v0

--- a/solution.py
+++ b/solution.py
@@ -262,7 +262,7 @@
 
 def vector_grads(links, sums):
     lengths = [v.shape[0] for v in sums]
-    total = lax.psum(jnp.concatenate(sums), AXES)
+    total = jnp.sum(lax.all_gather(jnp.concatenate(sums), AXES), axis=0)
     parts = []
     at = 0
     for length in lengths:

time: 580 us -> 565 us (0.974)
  blocking collectives: 40.1 us -> 0 us
  between operations: 11.6 us -> 25 us
  matrix products: 97.7 us -> 111 us
  waiting for transfers between devices: 260 us -> 252 us
    psum x1 -> x0, blocking collectives: 40.1 us -> none  [vector_grads(): total = lax.psum(jnp.concatenate(sums), AXES)]
    ppermute x57, waiting for transfers between devices: 260 us -> 252 us  [send(): return lax.ppermute(value, AXES, self.table(move))]
    dot_general x8, matrix products: 3.7 us -> 11 us  [scores_of(): jnp.einsum('qhe,khe->hqk', query, keys, preferred_element_type=f32)]
  transfers between devices with their start and end apart: 57 -> 58, of which waited for: 22 -> 21; matrix products, arithmetic and copies ran while one was open for 24% -> 25% of each run, Pallas kernels for 0% -> 0%
where the time goes in v1:
time: 565 us; the launch traced here: 554 us
  waiting for transfers between devices  252 us (45%)
  matrix products  111 us (20%)
  starting transfers between devices  63.7 us (11%)
  local copies, waits for them, and re-layouts  55.3 us (10%)
  other arithmetic  46.5 us (8%)
  between operations  25 us (4%)
    ppermute x57, waiting for transfers between devices, send(): return lax.ppermute(value, AXES, self.table(move))  252 us
    ppermute x57, starting transfers between devices, send(): return lax.ppermute(value, AXES, self.table(move))  63.7 us
    dot_general x8, matrix products, dot(): return jnp.dot(left, right, preferred_element_type=f32)  33.5 us
    dot_general x8, matrix products, dot_t(): lax.dot_general(left, right, (((1,), (1,)), ((), ())), preferred_element_...  19.4 us
    dot_general x32, matrix products, tdot(): lax.dot_general(left, right, (((0,), (0,)), ((), ())), preferred_element_...  18 us
    select_n x15, other arithmetic, pick(): return jnp.where(which == 0, zero, one)  16.5 us
    dynamic_update_slice x16, local copies, waits for them, and re-layouts, gather_other(): whole = lax.dynamic_update_slice_in_dim(whole, value, spot, 0)  13.5 us
  transfers between devices with their start and end apart: 58, of which 21 were waited for; matrix products, arithmetic and copies ran while one was open for 25% of the time, Pallas kernels for 0%

profile of v1, /device:TPU:0, one launch (start us, length us, event | category | flops | bytes accessed | tf_op | source)
XLA Modules:
  0.0 554.5 jit_solution(11278502881666388234)
XLA Ops:
  10.7 2.5 constant_dynamic-slice_fusion.1
  13.2 3.0 collective-permute-start.9
  17.0 2.3 constant_dynamic-slice_fusion.3
  19.3 2.0 collective-permute-start.1
  24.1 5.7 %fusion.200 = f32[256,2240]{1,0:T(8,128)} fusion(bf16[2240,1120]{1,0:T(8,128)(2,1)} %param.40, bf16[1,256,1120]{1,2,0:T(8,128)(2,1)S(1)} %copy-done.14), kind=kOutput, calls=%fused_computation.445 | convolution fusion | flops 1284505600 | bytes 7884800 | tf_op jit(solution)/shard_map/dot_general | solution.py:23
  37.2 36.3 %collective-permute-done = bf16[6720]{0:T(1024)(128)(2,1)S(1)} collective-permute-done((bf16[6720]{0:T(1024)(128)(2,1)S(1)}, bf16[6720]{0:T(1024)(128)(2,1)S(1)}, u32[]{:S(2)}, u32[]{:S(2)}) %collective-permute-start) | collective-permute-done | bytes 13472 | tf_op jit(solution)/shard_map/ppermute | solution.py:125
  74.8 4.1 fusion.169
  80.0 1.8 collective-permute-start.13
  87.6 6.1 %collective-permute-done.6 = bf16[18,8,1120]{2,1,0:T(8,128)(2,1)S(1)} collective-permute-done((bf16[18,8,1120]{2,1,0:T(8,128)(2,1)}, bf16[18,8,1120]{2,1,0:T(8,128)(2,1)S(1)}, u32[]{:S(2)}, u32[]{:S(2)}) %collective-permute-start.6) | collective-permute-done | bytes 322592 | tf_op jit(solution)/shard_map/ppermute | solution.py:125
  97.3 13.5 %collective-permute-done.13 = bf16[70,8,1120]{2,1,0:T(8,128)(2,1)S(1)} collective-permute-done((bf16[70,8,1120]{2,1,0:T(8,128)(2,1)S(1)}, bf16[70,8,1120]{2,1,0:T(8,128)(2,1)S(1)}, u32[]{:S(2)}, u32[]{:S(2)}) %collective-permute-start.13) | collective-permute-done | bytes 1254432 | tf_op jit(solution)/shard_map/ppermute | solution.py:125
  115.3 3.7 collective-permute-done.2
  119.8 26.9 %collective-permute-done.14 = bf16[70,8,1120]{2,1,0:T(8,128)(2,1)} collective-permute-done((bf16[70,8,1120]{2,1,0:T(8,128)(2,1)S(1)}, bf16[70,8,1120]{2,1,0:T(8,128)(2,1)}, u32[]{:S(2)}, u32[]{:S(2)}) %collective-permute-start.14) | collective-permute-done | bytes 1254432 | tf_op jit(solution)/shard_map/ppermute | solution.py:125
  148.5 25.5 %collective-permute-done.10 = bf16[18,8,4480]{2,1,0:T(8,128)(2,1)} collective-permute-done((bf16[18,8,4480]{2,1,0:T(8,128)(2,1)}, bf16[18,8,4480]{2,1,0:T(8,128)(2,1)}, u32[]{:S(2)}, u32[]{:S(2)}) %collective-permute-start.10) | collective-permute-done | bytes 1290272 | tf_op jit(solution)/shard_map/ppermute | solution.py:125
  175.6 2.1 convolution_add_fusion.1
  180.7 11.7 %while.28 = (s32[]{:T(128)}, bf16[4,256,5,56]{1,3,2,0:T(8,128)(2,1)S(1)}, f32[4,5,256,1]{2,1,3,0:T(8,128)S(1)}, bf16[4,256,5,56]{1,3,2,0:T(8,128)(2,1)}, bf16[4,...) while((s32[]{:T(128)}, ...), condition=%wide.region_5.6_spmd.clone, body=%wide.region_2.5_spmd.clone.sunk | while | flops 76354304 | bytes 4695385 | solution.py:65
  194.2 2.7 fusion.213
  198.0 2.7 constant_dynamic-update-slice_fusion.5
  200.8 4.1 fusion.163
  209.0 1.8 broadcast_select_fusion.5
  212.8 8.8 %convert_reduce_fusion = (f32[4480]{0:T(1024)S(1)}, bf16[256,4480]{1,0:T(8,128)(2,1)S(1)}, bf16[256,4480]{1,0:T(8,128)(2,1)}) fusion(f32[256,2240]{1,0:T(8,128)S(1)} %get-tuple-element.203, f32[256,2240]{1,0:T(8,128)S(1)} %get-tuple-element.202, f32[4480]{0:T(1024)S(1)} %maximum_convert_fusion, f32[256,4480]{1,0:T(8,128)} %fusion.163, ...), kind=kOutput, calls=%fused_computation.88 | convolution fusion | flops 1315610240 | bytes 19389440 | tf_op jit(solution)/shard_map/dot_general | solution.py:15
  221.7 1.8 broadcast_select_fusion.2
  234.3 31.7 %while.29 = (s32[]{:T(128)}, bf16[4,256,5,56]{1,3,2,0:T(8,128)(2,1)}, bf16[4,256,5,56]{1,3,2,0:T(8,128)(2,1)}, bf16[4,256,5,56]{1,3,2,0:T(8,128)(2,1)}, bf16[4,2...) while((s32[]{:T(128)}, ...), condition=%wide.region_12.13_spmd.clone, body=%wide.region_10.12_spmd.clone.sunk | while | flops 187069184 | bytes 11429233 | solution.py:88
  237.4 1.9 fusion.296
  240.3 1.9 fusion.297
  245.4 1.9 fusion.296
  248.2 1.9 fusion.297
  253.3 1.9 fusion.296
  256.1 1.9 fusion.297
  261.2 1.9 fusion.296
  264.0 1.9 fusion.297
  265.9 3.0 broadcast_select_fusion.6
  269.0 4.2 fusion.150
  275.3 2.6 copy.63
  278.5 3.6 broadcast_select_fusion.33
  284.8 3.0 add_bitcast_fusion
  287.9 5.7 %fusion.128 = f32[256,1120]{0,1:T(8,128)S(1)} fusion(bf16[2240,1120]{1,0:T(8,128)(2,1)} %param.40, pred[]{:T(512)S(6)} %eq.19, bf16[256,4480]{1,0:T(8,128)(2,1)} %get-tuple-element.206), kind=kOutput, calls=%fused_computation.196 | convolution fusion | flops 1285079040 | bytes 8667137 | tf_op jit(solution)/shard_map/dot_general | solution.py:15
  299.0 5.1 fusion.95
  304.1 4.1 collective-permute-done.31
  311.5 4.4 collective-permute-done.32
  316.8 3.5 collective-permute-start.33
  326.3 1.8 copy.57
  329.1 6.6 %collective-permute-done.34 = bf16[140,560]{1,0:T(8,128)(2,1)S(1)} collective-permute-done((bf16[140,560]{1,0:T(8,128)(2,1)S(1)}, bf16[140,560]{1,0:T(8,128)(2,1)S(1)}, u32[]{:S(2)}, u32[]{:S(2)}) %collective-permute-start.34) | collective-permute-done | bytes 156832 | tf_op jit(solution)/shard_map/ppermute | solution.py:125
  338.3 1.8 copy.60
  342.2 2.4 copy.64
  344.6 2.7 fusion.151
  351.4 9.2 %collective-permute-done.21 = bf16[2,420,560]{2,0,1:T(2,128)(2,1)} collective-permute-done((bf16[2,420,560]{2,0,1:T(2,128)(2,1)}, bf16[2,420,560]{2,0,1:T(2,128)(2,1)}, u32[]{:S(2)}, u32[]{:S(2)}) %collective-permute-start.21) | collective-permute-done | bytes 940832 | tf_op jit(solution)/shard_map/ppermute | solution.py:125
  360.6 3.4 fusion.209
  365.9 3.4 fusion.210
  373.1 25.1 %collective-permute-done.22 = bf16[420,560]{1,0:T(8,128)(2,1)S(1)} collective-permute-done((bf16[420,560]{1,0:T(8,128)(2,1)S(1)}, bf16[420,560]{1,0:T(8,128)(2,1)S(1)}, u32[]{:S(2)}, u32[]{:S(2)}) %collective-permute-start.22) | collective-permute-done | bytes 470432 | tf_op jit(solution)/shard_map/ppermute | solution.py:125
  399.3 3.3 collective-permute-start.23
  405.5 4.4 broadcast_select_fusion
  419.6 11.7 %collective-permute-done.24 = bf16[420,560]{1,0:T(8,128)(2,1)S(1)} collective-permute-done((bf16[420,560]{1,0:T(8,128)(2,1)S(1)}, bf16[420,560]{1,0:T(8,128)(2,1)S(1)}, u32[]{:S(2)}, u32[]{:S(2)}) %collective-permute-start.24) | collective-permute-done | bytes 470432 | tf_op jit(solution)/shard_map/ppermute | solution.py:125
  436.4 8.4 %collective-permute-done.51 = bf16[2,140,2240]{2,0,1:T(2,128)(2,1)S(1)} collective-permute-done((bf16[2,140,2240]{2,0,1:T(2,128)(2,1)S(1)}, bf16[2,140,2240]{2,0,1:T(2,128)(2,1)S(1)}, u32[]{:S(2)}, u32[]{:S(2)}) %collective-permute-start.51) | collective-permute-done | bytes 1254432 | tf_op jit(solution)/shard_map/ppermute | solution.py:125
  444.8 1.8 fusion.207
  448.0 15.3 %collective-permute-done.49 = bf16[2,140,2240]{2,0,1:T(2,128)(2,1)S(1)} collective-permute-done((bf16[2,140,2240]{2,0,1:T(2,128)(2,1)S(1)}, bf16[2,140,2240]{2,0,1:T(2,128)(2,1)S(1)}, u32[]{:S(2)}, u32[]{:S(2)}) %collective-permute-start.49) | collective-permute-done | bytes 1254432 | tf_op jit(solution)/shard_map/ppermute | solution.py:125
  463.3 1.8 fusion.208
  466.6 4.2 collective-permute-start.43
  472.1 5.1 collective-permute-done.52
  479.0 3.0 collective-permute-done.50
  482.7 1.9 collective-permute-start.53
  487.1 34.2 %collective-permute-done.44 = bf16[560,560]{1,0:T(8,128)(2,1)S(1)} collective-permute-done((bf16[560,560]{1,0:T(8,128)(2,1)S(1)}, bf16[560,560]{1,0:T(8,128)(2,1)S(1)}, u32[]{:S(2)}, u32[]{:S(2)}) %collective-permute-start.44) | collective-permute-done | bytes 627232 | tf_op jit(solution)/shard_map/ppermute | solution.py:125
  524.5 11.1 %collective-permute-done.54 = bf16[140,2240]{1,0:T(8,128)(2,1)S(1)} collective-permute-done((bf16[140,2240]{1,0:T(8,128)(2,1)S(1)}, bf16[140,2240]{1,0:T(8,128)(2,1)S(1)}, u32[]{:S(2)}, u32[]{:S(2)}) %collective-permute-start.54) | collective-permute-done | bytes 627232 | tf_op jit(solution)/shard_map/ppermute | solution.py:125
  538.0 2.1 collective-permute-start.56
  541.0 2.4 reduce_sum.218
  (392 shorter events, 150.1 us)
Async XLA Ops:
  7.2 533.8 %all-gather.4.cloned.1.call-start = ((), (), s32[]{:S(2)}) async-start(), calls=%async_computation | async-start | bytes 1774080 | tf_op jit(solution)/shard_map/all_gather | solution.py:265
  13.2 100.0 %collective-permute-start.9 = (bf16[18,8,4480]{2,1,0:T(8,128)(2,1)}, bf16[18,8,4480]{2,1,0:T(8,128)(2,1)}, u32[]{:S(2)}, u32[]{:S(2)}) collective-permute-start(bf16[18,8,4480]{2,1,0:T(8,128)(2,1)} %constant_dynamic-slice_fusion.1), channel_id=1, source_target_pairs={{0,1},{1,0},{2,3},{3,2},{4,5},{5,4},{6,7},{7,6},{8,9},{9,8},{10,11... | collective-permute-start | bytes 3870728 | tf_op jit(solution)/shard_map/ppermute | solution.py:125
  17.0 66.6 %collective-permute-start.5 = (bf16[18,8,1120]{2,1,0:T(8,128)(2,1)}, bf16[18,8,1120]{2,1,0:T(8,128)(2,1)}, u32[]{:S(2)}, u32[]{:S(2)}) collective-permute-start(bf16[18,8,1120]{2,1,0:T(8,128)(2,1)} %constant_dynamic-slice_fusion.2), channel_id=1, source_target_pairs={{0,1},{1,0},{2,3},{3,2},{4,5},{5,4},{6,7},{7,6},{8,9},{9,8},{10,11... | collective-permute-start | bytes 967688 | tf_op jit(solution)/shard_map/ppermute | solution.py:125
  19.3 74.5 %collective-permute-start.1 = (bf16[18,8,3360]{2,1,0:T(8,128)(2,1)}, bf16[18,8,3360]{2,1,0:T(8,128)(2,1)}, u32[]{:S(2)}, u32[]{:S(2)}) collective-permute-start(bf16[18,8,3360]{2,1,0:T(8,128)(2,1)} %constant_dynamic-slice_fusion.3), channel_id=1, source_target_pairs={{0,1},{1,0},{2,3},{3,2},{4,5},{5,4},{6,7},{7,6},{8,9},{9,8},{10,11... | collective-permute-start | bytes 2903048 | tf_op jit(solution)/shard_map/ppermute | solution.py:125
  21.5 52.0 %collective-permute-start = (bf16[6720]{0:T(1024)(128)(2,1)S(1)}, bf16[6720]{0:T(1024)(128)(2,1)S(1)}, u32[]{:S(2)}, u32[]{:S(2)}) collective-permute-start(bf16[6720]{0:T(1024)(128)(2,1)S(1)} %concatenate.120), channel_id=1, source_target_pairs={{0,1},{1,0},{2,3},{3,2},{4,5},{5,4},{6,7},{7,6},{8,9},{9,8},{10,11... | collective-permute-start | bytes 40328 | tf_op jit(solution)/shard_map/ppermute | solution.py:125
  22.4 57.6 %collective-permute-start.47 = (bf16[256,560]{0,1:T(8,128)(2,1)}, bf16[256,560]{0,1:T(8,128)(2,1)S(1)}, u32[]{:S(2)}, u32[]{:S(2)}) collective-permute-start(bf16[256,560]{0,1:T(8,128)(2,1)} %get-tuple-element.251), channel_id=1, source_target_pairs={{0,2},{1,3},{2,0},{3,1},{4,6},{5,7},{6,4},{7,5},{8,10},{9,11},{10,... | collective-permute-start | bytes 860168 | tf_op jit(solution)/shard_map/ppermute | solution.py:125
  22.8 51.6 %copy-start.37 = (f32[256]{0:T(256)}, f32[256]{0:T(256)S(1)}, u32[]{:S(2)}) copy-start(f32[256]{0:T(256)S(1)} %fusion.195) | copy-start | bytes 3076
  29.8 43.8 %copy-start.48 = (bf16[560]{0:T(1024)(128)(2,1)S(1)}, bf16[560]{0:T(1024)(128)(2,1)}, u32[]{:S(2)}) copy-start(bf16[560]{0:T(1024)(128)(2,1)} %param.29) | copy-start | bytes 3364
  78.9 7.3 %collective-permute-start.18 = (bf16[256,1120]{0,1:T(8,128)(2,1)S(1)}, bf16[256,1120]{0,1:T(8,128)(2,1)S(1)}, u32[]{:S(2)}, u32[]{:S(2)}) collective-permute-start(bf16[256,1120]{0,1:T(8,128)(2,1)S(1)} %fusion.139), channel_id=1, source_target_pairs={{0,2},{1,3},{2,0},{3,1},{4,6},{5,7},{6,4},{7,5},{8,10},{9,11},{10,... | collective-permute-start | bytes 1720328 | tf_op jit(solution)/shard_map/ppermute | solution.py:125
  80.0 30.8 %collective-permute-start.13 = (bf16[70,8,1120]{2,1,0:T(8,128)(2,1)S(1)}, bf16[70,8,1120]{2,1,0:T(8,128)(2,1)S(1)}, u32[]{:S(2)}, u32[]{:S(2)}) collective-permute-start(bf16[70,8,1120]{2,1,0:T(8,128)(2,1)S(1)} %constant_dynamic-slice_fusion), channel_id=1, source_target_pairs={{0,1},{1,0},{2,3},{3,2},{4,5},{5,4},{6,7},{7,6},{8,9},{9,8},{10,11... | collective-permute-start | bytes 3763208 | tf_op jit(solution)/shard_map/ppermute | solution.py:125
  83.6 10.1 %collective-permute-start.6 = (bf16[18,8,1120]{2,1,0:T(8,128)(2,1)}, bf16[18,8,1120]{2,1,0:T(8,128)(2,1)S(1)}, u32[]{:S(2)}, u32[]{:S(2)}) collective-permute-start(bf16[18,8,1120]{2,1,0:T(8,128)(2,1)} %collective-permute-done.5), channel_id=1, source_target_pairs={{0,4},{1,5},{2,6},{3,7},{4,0},{5,1},{6,2},{7,3},{8,12},{9,13},{10,... | collective-permute-start | bytes 967688 | tf_op jit(solution)/shard_map/ppermute | solution.py:125
  86.2 7.5 %collective-permute-start.7 = (bf16[18,8,1120]{2,1,0:T(8,128)(2,1)}, bf16[18,8,1120]{2,1,0:T(8,128)(2,1)S(1)}, u32[]{:S(2)}, u32[]{:S(2)}) collective-permute-start(bf16[18,8,1120]{2,1,0:T(8,128)(2,1)} %collective-permute-done.5), channel_id=1, source_target_pairs={{0,2},{1,3},{2,0},{3,1},{4,6},{5,7},{6,4},{7,5},{8,10},{9,11},{10,... | collective-permute-start | bytes 967688 | tf_op jit(solution)/shard_map/ppermute | solution.py:125
  93.7 3.5 collective-permute-start.8
  93.8 25.2 %collective-permute-start.2 = (bf16[18,8,3360]{2,1,0:T(8,128)(2,1)}, bf16[18,8,3360]{2,1,0:T(8,128)(2,1)S(1)}, u32[]{:S(2)}, u32[]{:S(2)}) collective-permute-start(bf16[18,8,3360]{2,1,0:T(8,128)(2,1)} %collective-permute-done.1), channel_id=1, source_target_pairs={{0,4},{1,5},{2,6},{3,7},{4,0},{5,1},{6,2},{7,3},{8,12},{9,13},{10,... | collective-permute-start | bytes 2903048 | tf_op jit(solution)/shard_map/ppermute | solution.py:125
  95.4 23.7 %collective-permute-start.3 = (bf16[18,8,3360]{2,1,0:T(8,128)(2,1)}, bf16[18,8,3360]{2,1,0:T(8,128)(2,1)S(1)}, u32[]{:S(2)}, u32[]{:S(2)}) collective-permute-start(bf16[18,8,3360]{2,1,0:T(8,128)(2,1)} %collective-permute-done.1), channel_id=1, source_target_pairs={{0,2},{1,3},{2,0},{3,1},{4,6},{5,7},{6,4},{7,5},{8,10},{9,11},{10,... | collective-permute-start | bytes 2903048 | tf_op jit(solution)/shard_map/ppermute | solution.py:125
  97.3 15.3 %copy-start.25 = (bf16[70,8,1120]{2,1,0:T(8,128)(2,1)}, bf16[70,8,1120]{2,1,0:T(8,128)(2,1)S(1)}, u32[]{:S(2)}) copy-start(bf16[70,8,1120]{2,1,0:T(8,128)(2,1)S(1)} %constant_dynamic-update-slice_fusion.8) | copy-start | bytes 3763204
  110.8 35.9 %collective-permute-start.14 = (bf16[70,8,1120]{2,1,0:T(8,128)(2,1)S(1)}, bf16[70,8,1120]{2,1,0:T(8,128)(2,1)}, u32[]{:S(2)}, u32[]{:S(2)}) collective-permute-start(bf16[70,8,1120]{2,1,0:T(8,128)(2,1)S(1)} %collective-permute-done.13), channel_id=1, source_target_pairs={{0,4},{1,5},{2,6},{3,7},{4,0},{5,1},{6,2},{7,3},{8,12},{9,13},{10,... | collective-permute-start | bytes 3763208 | tf_op jit(solution)/shard_map/ppermute | solution.py:125
  112.6 35.7 %collective-permute-start.15 = (bf16[70,8,1120]{2,1,0:T(8,128)(2,1)S(1)}, bf16[70,8,1120]{2,1,0:T(8,128)(2,1)S(1)}, u32[]{:S(2)}, u32[]{:S(2)}) collective-permute-start(bf16[70,8,1120]{2,1,0:T(8,128)(2,1)S(1)} %collective-permute-done.13), channel_id=1, source_target_pairs={{0,2},{1,3},{2,0},{3,1},{4,6},{5,7},{6,4},{7,5},{8,10},{9,11},{10,... | collective-permute-start | bytes 3763208 | tf_op jit(solution)/shard_map/ppermute | solution.py:125
  113.2 60.8 %collective-permute-start.10 = (bf16[18,8,4480]{2,1,0:T(8,128)(2,1)}, bf16[18,8,4480]{2,1,0:T(8,128)(2,1)}, u32[]{:S(2)}, u32[]{:S(2)}) collective-permute-start(bf16[18,8,4480]{2,1,0:T(8,128)(2,1)} %collective-permute-done.9), channel_id=1, source_target_pairs={{0,4},{1,5},{2,6},{3,7},{4,0},{5,1},{6,2},{7,3},{8,12},{9,13},{10,... | collective-permute-start | bytes 3870728 | tf_op jit(solution)/shard_map/ppermute | solution.py:125
  119.0 79.1 %collective-permute-start.11 = (bf16[18,8,4480]{2,1,0:T(8,128)(2,1)}, bf16[18,8,4480]{2,1,0:T(8,128)(2,1)}, u32[]{:S(2)}, u32[]{:S(2)}) collective-permute-start(bf16[18,8,4480]{2,1,0:T(8,128)(2,1)} %collective-permute-done.9), channel_id=1, source_target_pairs={{0,2},{1,3},{2,0},{3,1},{4,6},{5,7},{6,4},{7,5},{8,10},{9,11},{10,... | collective-permute-start | bytes 3870728 | tf_op jit(solution)/shard_map/ppermute | solution.py:125
  119.1 56.3 %collective-permute-start.4 = (bf16[18,8,3360]{2,1,0:T(8,128)(2,1)S(1)}, bf16[18,8,3360]{2,1,0:T(8,128)(2,1)S(1)}, u32[]{:S(2)}, u32[]{:S(2)}) collective-permute-start(bf16[18,8,3360]{2,1,0:T(8,128)(2,1)S(1)} %collective-permute-done.2), channel_id=1, source_target_pairs={{0,2},{1,3},{2,0},{3,1},{4,6},{5,7},{6,4},{7,5},{8,10},{9,11},{10,... | collective-permute-start | bytes 2903048 | tf_op jit(solution)/shard_map/ppermute | solution.py:125
  146.7 60.6 %collective-permute-start.16 = (bf16[70,8,1120]{2,1,0:T(8,128)(2,1)}, bf16[70,8,1120]{2,1,0:T(8,128)(2,1)}, u32[]{:S(2)}, u32[]{:S(2)}) collective-permute-start(bf16[70,8,1120]{2,1,0:T(8,128)(2,1)} %collective-permute-done.14), channel_id=1, source_target_pairs={{0,2},{1,3},{2,0},{3,1},{4,6},{5,7},{6,4},{7,5},{8,10},{9,11},{10,... | collective-permute-start | bytes 3763208 | tf_op jit(solution)/shard_map/ppermute | solution.py:125
  148.4 29.2 %copy-start.2 = (bf16[280,8,1120]{2,1,0:T(8,128)(2,1)}, bf16[280,8,1120]{2,1,0:T(8,128)(2,1)S(1)}, u32[]{:S(2)}) copy-start(bf16[280,8,1120]{2,1,0:T(8,128)(2,1)S(1)} %constant_dynamic-update-slice_fusion.1) | copy-start | bytes 15052804
  173.9 37.4 %collective-permute-start.12 = (bf16[18,8,4480]{2,1,0:T(8,128)(2,1)}, bf16[18,8,4480]{2,1,0:T(8,128)(2,1)}, u32[]{:S(2)}, u32[]{:S(2)}) collective-permute-start(bf16[18,8,4480]{2,1,0:T(8,128)(2,1)} %collective-permute-done.10), channel_id=1, source_target_pairs={{0,2},{1,3},{2,0},{3,1},{4,6},{5,7},{6,4},{7,5},{8,10},{9,11},{10,... | collective-permute-start | bytes 3870728 | tf_op jit(solution)/shard_map/ppermute | solution.py:125
  197.5 7.4 %collective-permute-start.38 = (bf16[256,1120]{0,1:T(8,128)(2,1)S(1)}, bf16[256,1120]{0,1:T(8,128)(2,1)S(1)}, u32[]{:S(2)}, u32[]{:S(2)}) collective-permute-start(bf16[256,1120]{0,1:T(8,128)(2,1)S(1)} %add_convert_fusion), channel_id=1, source_target_pairs={{0,2},{1,3},{2,0},{3,1},{4,6},{5,7},{6,4},{7,5},{8,10},{9,11},{10,... | collective-permute-start | bytes 1720328 | tf_op jit(solution)/shard_map/ppermute | solution.py:125
  200.7 5.3 collective-permute-start.28
  274.7 129.2 %collective-permute-start.48 = (bf16[256,4480]{1,0:T(8,128)(2,1)}, bf16[256,4480]{1,0:T(8,128)(2,1)}, u32[]{:S(2)}, u32[]{:S(2)}) collective-permute-start(bf16[256,4480]{1,0:T(8,128)(2,1)} %get-tuple-element.206), channel_id=1, source_target_pairs={{0,2},{1,3},{2,0},{3,1},{4,6},{5,7},{6,4},{7,5},{8,10},{9,11},{10,... | collective-permute-start | bytes 6881288 | tf_op jit(solution)/shard_map/ppermute | solution.py:125
  277.8 64.3 %collective-permute-start.37 = (bf16[256,2240]{0,1:T(8,128)(2,1)}, bf16[256,2240]{0,1:T(8,128)(2,1)}, u32[]{:S(2)}, u32[]{:S(2)}) collective-permute-start(bf16[256,2240]{0,1:T(8,128)(2,1)} %copy.63), channel_id=1, source_target_pairs={{0,2},{1,3},{2,0},{3,1},{4,6},{5,7},{6,4},{7,5},{8,10},{9,11},{10,... | collective-permute-start | bytes 3440648 | tf_op jit(solution)/shard_map/ppermute | solution.py:125
  277.9 15.7 %collective-permute-start.27 = (bf16[256,560]{0,1:T(8,128)(2,1)}, bf16[256,560]{0,1:T(8,128)(2,1)}, u32[]{:S(2)}, u32[]{:S(2)}) collective-permute-start(bf16[256,560]{0,1:T(8,128)(2,1)} %get-tuple-element.257), channel_id=1, source_target_pairs={{0,2},{1,3},{2,0},{3,1},{4,6},{5,7},{6,4},{7,5},{8,10},{9,11},{10,... | collective-permute-start | bytes 860168 | tf_op jit(solution)/shard_map/ppermute | solution.py:125
  278.4 43.2 %collective-permute-start.17 = (bf16[256,1680]{0,1:T(8,128)(2,1)}, bf16[256,1680]{0,1:T(8,128)(2,1)}, u32[]{:S(2)}, u32[]{:S(2)}) collective-permute-start(bf16[256,1680]{0,1:T(8,128)(2,1)} %get-tuple-element.225), channel_id=1, source_target_pairs={{0,2},{1,3},{2,0},{3,1},{4,6},{5,7},{6,4},{7,5},{8,10},{9,11},{10,... | collective-permute-start | bytes 2580488 | tf_op jit(solution)/shard_map/ppermute | solution.py:125
  284.8 14.1 %slice-start.2 = ((s8[5160960]{0:T(1024)(128)(4,1)}), s8[4194304]{0:T(1024)(128)(4,1)S(1)}, s32[]{:S(2)}) async-start(s8[5160960]{0:T(1024)(128)(4,1)} %bitcast.402), calls=%async_computation.3 | async-start | bytes 8388608
  287.9 11.1 %slice-start.3 = ((s8[5160960]{0:T(1024)(128)(4,1)}), s8[966656]{0:T(1024)(128)(4,1)S(1)}, s32[]{:S(2)}) async-start(s8[5160960]{0:T(1024)(128)(4,1)} %bitcast.402), calls=%async_computation.4 | async-start | bytes 1933312
  295.6 14.0 %collective-permute-start.29 = (bf16[2,140,560]{2,1,0:T(8,128)(2,1)S(1)}, bf16[2,140,560]{2,1,0:T(8,128)(2,1)S(1)}, u32[]{:S(2)}, u32[]{:S(2)}) collective-permute-start(bf16[2,140,560]{2,1,0:T(8,128)(2,1)S(1)} %pad_maximum_fusion.20), channel_id=1, source_target_pairs={{0,1},{1,0},{2,3},{3,2},{4,5},{5,4},{6,7},{7,6},{8,9},{9,8},{10,11... | collective-permute-start | bytes 940808 | tf_op jit(solution)/shard_map/ppermute | solution.py:125
  297.4 10.7 %collective-permute-start.31 = (bf16[2,140,560]{2,1,0:T(8,128)(2,1)S(1)}, bf16[2,140,560]{2,1,0:T(8,128)(2,1)S(1)}, u32[]{:S(2)}, u32[]{:S(2)}) collective-permute-start(bf16[2,140,560]{2,1,0:T(8,128)(2,1)S(1)} %pad_maximum_fusion.21), channel_id=1, source_target_pairs={{0,4},{1,5},{2,6},{3,7},{4,0},{5,1},{6,2},{7,3},{8,12},{9,13},{10,... | collective-permute-start | bytes 940808 | tf_op jit(solution)/shard_map/ppermute | solution.py:125
  308.5 7.4 %collective-permute-start.32 = (bf16[140,560]{1,0:T(8,128)(2,1)S(1)}, bf16[140,560]{1,0:T(8,128)(2,1)S(1)}, u32[]{:S(2)}, u32[]{:S(2)}) collective-permute-start(bf16[140,560]{1,0:T(8,128)(2,1)S(1)} %fusion.133), channel_id=1, source_target_pairs={{0,1},{1,0},{2,3},{3,2},{4,5},{5,4},{6,7},{7,6},{8,9},{9,8},{10,11... | collective-permute-start | bytes 470408 | tf_op jit(solution)/shard_map/ppermute | solution.py:125
  310.0 6.4 %collective-permute-start.30 = (bf16[140,560]{1,0:T(8,128)(2,1)S(1)}, bf16[140,560]{1,0:T(8,128)(2,1)S(1)}, u32[]{:S(2)}, u32[]{:S(2)}) collective-permute-start(bf16[140,560]{1,0:T(8,128)(2,1)S(1)} %fusion.132), channel_id=1, source_target_pairs={{0,4},{1,5},{2,6},{3,7},{4,0},{5,1},{6,2},{7,3},{8,12},{9,13},{10,... | collective-permute-start | bytes 470408 | tf_op jit(solution)/shard_map/ppermute | solution.py:125
  316.8 11.3 %collective-permute-start.33 = (bf16[140,560]{1,0:T(8,128)(2,1)S(1)}, bf16[140,560]{1,0:T(8,128)(2,1)S(1)}, u32[]{:S(2)}, u32[]{:S(2)}) collective-permute-start(bf16[140,560]{1,0:T(8,128)(2,1)S(1)} %get-tuple-element.246), channel_id=1, source_target_pairs={{0,8},{1,9},{4,12},{5,13},{8,0},{9,1},{12,4},{13,5},{18,26},{19,27... | collective-permute-start | bytes 470408 | tf_op jit(solution)/shard_map/ppermute | solution.py:125
  320.3 15.4 %collective-permute-start.35 = (bf16[140,560]{1,0:T(8,128)(2,1)S(1)}, bf16[140,560]{1,0:T(8,128)(2,1)S(1)}, u32[]{:S(2)}, u32[]{:S(2)}) collective-permute-start(bf16[140,560]{1,0:T(8,128)(2,1)S(1)} %get-tuple-element.246), channel_id=1, source_target_pairs={{2,26},{3,27},{6,30},{7,31},{10,18},{11,19},{14,22},{15,23},{16,8}... | collective-permute-start | bytes 470408 | tf_op jit(solution)/shard_map/ppermute | solution.py:125
  321.6 14.1 %collective-permute-start.34 = (bf16[140,560]{1,0:T(8,128)(2,1)S(1)}, bf16[140,560]{1,0:T(8,128)(2,1)S(1)}, u32[]{:S(2)}, u32[]{:S(2)}) collective-permute-start(bf16[140,560]{1,0:T(8,128)(2,1)S(1)} %get-tuple-element.245), channel_id=1, source_target_pairs={{2,18},{3,19},{6,22},{7,23},{10,26},{11,27},{14,30},{15,31},{16,0}... | collective-permute-start | bytes 470408 | tf_op jit(solution)/shard_map/ppermute | solution.py:125
  328.1 37.7 %collective-permute-start.19 = (bf16[2,420,560]{2,0,1:T(2,128)(2,1)}, bf16[2,420,560]{2,0,1:T(2,128)(2,1)}, u32[]{:S(2)}, u32[]{:S(2)}) collective-permute-start(bf16[2,420,560]{2,0,1:T(2,128)(2,1)} %copy.57), channel_id=1, source_target_pairs={{0,1},{1,0},{2,3},{3,2},{4,5},{5,4},{6,7},{7,6},{8,9},{9,8},{10,11... | collective-permute-start | bytes 2822408 | tf_op jit(solution)/shard_map/ppermute | solution.py:125
  335.8 5.6 %collective-permute-start.36 = (f32[70,560]{1,0:T(8,128)S(1)}, f32[70,560]{1,0:T(8,128)S(1)}, u32[]{:S(2)}, u32[]{:S(2)}) collective-permute-start(f32[70,560]{1,0:T(8,128)S(1)} %slice_select_fusion.3), channel_id=1, source_target_pairs={{0,2},{1,3},{4,6},{5,7},{8,10},{9,11},{12,14},{13,15},{18,16},{19,... | collective-permute-start | bytes 470408 | tf_op jit(solution)/shard_map/ppermute | solution.py:125
  340.1 20.5 %collective-permute-start.21 = (bf16[2,420,560]{2,0,1:T(2,128)(2,1)}, bf16[2,420,560]{2,0,1:T(2,128)(2,1)}, u32[]{:S(2)}, u32[]{:S(2)}) collective-permute-start(bf16[2,420,560]{2,0,1:T(2,128)(2,1)} %copy.60), channel_id=1, source_target_pairs={{0,4},{1,5},{2,6},{3,7},{4,0},{5,1},{6,2},{7,3},{8,12},{9,13},{10,... | collective-permute-start | bytes 2822408 | tf_op jit(solution)/shard_map/ppermute | solution.py:125
  349.1 67.5 %collective-permute-start.39 = (bf16[2,560,560]{2,1,0:T(8,128)(2,1)S(1)}, bf16[2,560,560]{2,1,0:T(8,128)(2,1)S(1)}, u32[]{:S(2)}, u32[]{:S(2)}) collective-permute-start(bf16[2,560,560]{2,1,0:T(8,128)(2,1)S(1)} %pad_maximum_fusion.3), channel_id=1, source_target_pairs={{0,1},{1,0},{2,3},{3,2},{4,5},{5,4},{6,7},{7,6},{8,9},{9,8},{10,11... | collective-permute-start | bytes 3763208 | tf_op jit(solution)/shard_map/ppermute | solution.py:125
  364.5 33.6 %collective-permute-start.22 = (bf16[420,560]{1,0:T(8,128)(2,1)S(1)}, bf16[420,560]{1,0:T(8,128)(2,1)S(1)}, u32[]{:S(2)}, u32[]{:S(2)}) collective-permute-start(bf16[420,560]{1,0:T(8,128)(2,1)S(1)} %fusion.111), channel_id=1, source_target_pairs={{0,1},{1,0},{2,3},{3,2},{4,5},{5,4},{6,7},{7,6},{8,9},{9,8},{10,11... | collective-permute-start | bytes 1411208 | tf_op jit(solution)/shard_map/ppermute | solution.py:125
  369.9 28.8 %collective-permute-start.20 = (bf16[420,560]{1,0:T(8,128)(2,1)S(1)}, bf16[420,560]{1,0:T(8,128)(2,1)S(1)}, u32[]{:S(2)}, u32[]{:S(2)}) collective-permute-start(bf16[420,560]{1,0:T(8,128)(2,1)S(1)} %fusion.110), channel_id=1, source_target_pairs={{0,4},{1,5},{2,6},{3,7},{4,0},{5,1},{6,2},{7,3},{8,12},{9,13},{10,... | collective-permute-start | bytes 1411208 | tf_op jit(solution)/shard_map/ppermute | solution.py:125
  372.2 42.1 %collective-permute-start.41 = (bf16[2,560,560]{2,1,0:T(8,128)(2,1)S(1)}, bf16[2,560,560]{2,1,0:T(8,128)(2,1)S(1)}, u32[]{:S(2)}, u32[]{:S(2)}) collective-permute-start(bf16[2,560,560]{2,1,0:T(8,128)(2,1)S(1)} %pad_maximum_fusion.4), channel_id=1, source_target_pairs={{0,4},{1,5},{2,6},{3,7},{4,0},{5,1},{6,2},{7,3},{8,12},{9,13},{10,... | collective-permute-start | bytes 3763208 | tf_op jit(solution)/shard_map/ppermute | solution.py:125
  399.3 18.8 %collective-permute-start.23 = (bf16[420,560]{1,0:T(8,128)(2,1)S(1)}, bf16[420,560]{1,0:T(8,128)(2,1)S(1)}, u32[]{:S(2)}, u32[]{:S(2)}) collective-permute-start(bf16[420,560]{1,0:T(8,128)(2,1)S(1)} %get-tuple-element.220), channel_id=1, source_target_pairs={{0,8},{1,9},{4,12},{5,13},{8,0},{9,1},{12,4},{13,5},{18,26},{19,27... | collective-permute-start | bytes 1411208 | tf_op jit(solution)/shard_map/ppermute | solution.py:125
  402.6 30.4 %collective-permute-start.25 = (bf16[420,560]{1,0:T(8,128)(2,1)S(1)}, bf16[420,560]{1,0:T(8,128)(2,1)S(1)}, u32[]{:S(2)}, u32[]{:S(2)}) collective-permute-start(bf16[420,560]{1,0:T(8,128)(2,1)S(1)} %get-tuple-element.220), channel_id=1, source_target_pairs={{2,26},{3,27},{6,30},{7,31},{10,18},{11,19},{14,22},{15,23},{16,8}... | collective-permute-start | bytes 1411208 | tf_op jit(solution)/shard_map/ppermute | solution.py:125
  403.9 27.5 %collective-permute-start.24 = (bf16[420,560]{1,0:T(8,128)(2,1)S(1)}, bf16[420,560]{1,0:T(8,128)(2,1)S(1)}, u32[]{:S(2)}, u32[]{:S(2)}) collective-permute-start(bf16[420,560]{1,0:T(8,128)(2,1)S(1)} %get-tuple-element.219), channel_id=1, source_target_pairs={{2,18},{3,19},{6,22},{7,23},{10,26},{11,27},{14,30},{15,31},{16,0}... | collective-permute-start | bytes 1411208 | tf_op jit(solution)/shard_map/ppermute | solution.py:125
  414.3 30.5 %collective-permute-start.51 = (bf16[2,140,2240]{2,0,1:T(2,128)(2,1)S(1)}, bf16[2,140,2240]{2,0,1:T(2,128)(2,1)S(1)}, u32[]{:S(2)}, u32[]{:S(2)}) collective-permute-start(bf16[2,140,2240]{2,0,1:T(2,128)(2,1)S(1)} %copy.68), channel_id=1, source_target_pairs={{0,4},{1,5},{2,6},{3,7},{4,0},{5,1},{6,2},{7,3},{8,12},{9,13},{10,... | collective-permute-start | bytes 3763208 | tf_op jit(solution)/shard_map/ppermute | solution.py:125
  416.7 19.0 %collective-permute-start.42 = (bf16[560,560]{1,0:T(8,128)(2,1)S(1)}, bf16[560,560]{1,0:T(8,128)(2,1)S(1)}, u32[]{:S(2)}, u32[]{:S(2)}) collective-permute-start(bf16[560,560]{1,0:T(8,128)(2,1)S(1)} %fusion.109), channel_id=1, source_target_pairs={{0,1},{1,0},{2,3},{3,2},{4,5},{5,4},{6,7},{7,6},{8,9},{9,8},{10,11... | collective-permute-start | bytes 1881608 | tf_op jit(solution)/shard_map/ppermute | solution.py:125
  418.1 45.2 %collective-permute-start.49 = (bf16[2,140,2240]{2,0,1:T(2,128)(2,1)S(1)}, bf16[2,140,2240]{2,0,1:T(2,128)(2,1)S(1)}, u32[]{:S(2)}, u32[]{:S(2)}) collective-permute-start(bf16[2,140,2240]{2,0,1:T(2,128)(2,1)S(1)} %copy.65), channel_id=1, source_target_pairs={{0,1},{1,0},{2,3},{3,2},{4,5},{5,4},{6,7},{7,6},{8,9},{9,8},{10,11... | collective-permute-start | bytes 3763208 | tf_op jit(solution)/shard_map/ppermute | solution.py:125
  431.4 34.4 %collective-permute-start.40 = (bf16[560,560]{1,0:T(8,128)(2,1)S(1)}, bf16[560,560]{1,0:T(8,128)(2,1)S(1)}, u32[]{:S(2)}, u32[]{:S(2)}) collective-permute-start(bf16[560,560]{1,0:T(8,128)(2,1)S(1)} %fusion.108), channel_id=1, source_target_pairs={{0,4},{1,5},{2,6},{3,7},{4,0},{5,1},{6,2},{7,3},{8,12},{9,13},{10,... | collective-permute-start | bytes 1881608 | tf_op jit(solution)/shard_map/ppermute | solution.py:125
  433.3 106.8 %collective-permute-start.26 = (f32[210,560]{1,0:T(8,128)S(1)}, f32[210,560]{1,0:T(8,128)S(1)}, u32[]{:S(2)}, u32[]{:S(2)}) collective-permute-start(f32[210,560]{1,0:T(8,128)S(1)} %slice_select_fusion.2), channel_id=1, source_target_pairs={{0,2},{1,3},{4,6},{5,7},{8,10},{9,11},{12,14},{13,15},{18,16},{19,... | collective-permute-start | bytes 1411208 | tf_op jit(solution)/shard_map/ppermute | solution.py:125
  447.1 30.1 %collective-permute-start.52 = (bf16[140,2240]{1,0:T(8,128)(2,1)S(1)}, bf16[140,2240]{1,0:T(8,128)(2,1)S(1)}, u32[]{:S(2)}, u32[]{:S(2)}) collective-permute-start(bf16[140,2240]{1,0:T(8,128)(2,1)S(1)} %fusion.76), channel_id=1, source_target_pairs={{0,1},{1,0},{2,3},{3,2},{4,5},{5,4},{6,7},{7,6},{8,9},{9,8},{10,11... | collective-permute-start | bytes 1881608 | tf_op jit(solution)/shard_map/ppermute | solution.py:125
  465.6 16.4 %collective-permute-start.50 = (bf16[140,2240]{1,0:T(8,128)(2,1)S(1)}, bf16[140,2240]{1,0:T(8,128)(2,1)S(1)}, u32[]{:S(2)}, u32[]{:S(2)}) collective-permute-start(bf16[140,2240]{1,0:T(8,128)(2,1)S(1)} %fusion.75), channel_id=1, source_target_pairs={{0,4},{1,5},{2,6},{3,7},{4,0},{5,1},{6,2},{7,3},{8,12},{9,13},{10,... | collective-permute-start | bytes 1881608 | tf_op jit(solution)/shard_map/ppermute | solution.py:125
  466.6 19.3 %collective-permute-start.43 = (bf16[560,560]{1,0:T(8,128)(2,1)S(1)}, bf16[560,560]{1,0:T(8,128)(2,1)S(1)}, u32[]{:S(2)}, u32[]{:S(2)}) collective-permute-start(bf16[560,560]{1,0:T(8,128)(2,1)S(1)} %get-tuple-element.210), channel_id=1, source_target_pairs={{0,8},{1,9},{4,12},{5,13},{8,0},{9,1},{12,4},{13,5},{18,26},{19,27... | collective-permute-start | bytes 1881608 | tf_op jit(solution)/shard_map/ppermute | solution.py:125
  470.8 51.9 %collective-permute-start.45 = (bf16[560,560]{1,0:T(8,128)(2,1)S(1)}, bf16[560,560]{1,0:T(8,128)(2,1)S(1)}, u32[]{:S(2)}, u32[]{:S(2)}) collective-permute-start(bf16[560,560]{1,0:T(8,128)(2,1)S(1)} %get-tuple-element.210), channel_id=1, source_target_pairs={{2,26},{3,27},{6,30},{7,31},{10,18},{11,19},{14,22},{15,23},{16,8}... | collective-permute-start | bytes 1881608 | tf_op jit(solution)/shard_map/ppermute | solution.py:125
  477.2 44.2 %collective-permute-start.44 = (bf16[560,560]{1,0:T(8,128)(2,1)S(1)}, bf16[560,560]{1,0:T(8,128)(2,1)S(1)}, u32[]{:S(2)}, u32[]{:S(2)}) collective-permute-start(bf16[560,560]{1,0:T(8,128)(2,1)S(1)} %get-tuple-element.209), channel_id=1, source_target_pairs={{2,18},{3,19},{6,22},{7,23},{10,26},{11,27},{14,30},{15,31},{16,0}... | collective-permute-start | bytes 1881608 | tf_op jit(solution)/shard_map/ppermute | solution.py:125
  482.7 41.8 %collective-permute-start.53 = (bf16[140,2240]{1,0:T(8,128)(2,1)S(1)}, bf16[140,2240]{1,0:T(8,128)(2,1)S(1)}, u32[]{:S(2)}, u32[]{:S(2)}) collective-permute-start(bf16[140,2240]{1,0:T(8,128)(2,1)S(1)} %get-tuple-element.212), channel_id=1, source_target_pairs={{0,8},{1,9},{4,12},{5,13},{8,0},{9,1},{12,4},{13,5},{18,26},{19,27... | collective-permute-start | bytes 1881608 | tf_op jit(solution)/shard_map/ppermute | solution.py:125
  485.8 49.8 %collective-permute-start.55 = (bf16[140,2240]{1,0:T(8,128)(2,1)S(1)}, bf16[140,2240]{1,0:T(8,128)(2,1)S(1)}, u32[]{:S(2)}, u32[]{:S(2)}) collective-permute-start(bf16[140,2240]{1,0:T(8,128)(2,1)S(1)} %get-tuple-element.212), channel_id=1, source_target_pairs={{2,26},{3,27},{6,30},{7,31},{10,18},{11,19},{14,22},{15,23},{16,8}... | collective-permute-start | bytes 1881608 | tf_op jit(solution)/shard_map/ppermute | solution.py:125
  521.4 14.2 %collective-permute-start.54 = (bf16[140,2240]{1,0:T(8,128)(2,1)S(1)}, bf16[140,2240]{1,0:T(8,128)(2,1)S(1)}, u32[]{:S(2)}, u32[]{:S(2)}) collective-permute-start(bf16[140,2240]{1,0:T(8,128)(2,1)S(1)} %get-tuple-element.211), channel_id=1, source_target_pairs={{2,18},{3,19},{6,22},{7,23},{10,26},{11,27},{14,30},{15,31},{16,0}... | collective-permute-start | bytes 1881608 | tf_op jit(solution)/shard_map/ppermute | solution.py:125
  523.2 21.7 %collective-permute-start.46 = (f32[280,560]{1,0:T(8,128)S(1)}, f32[280,560]{1,0:T(8,128)S(1)}, u32[]{:S(2)}, u32[]{:S(2)}) collective-permute-start(f32[280,560]{1,0:T(8,128)S(1)} %slice_select_fusion), channel_id=1, source_target_pairs={{0,2},{1,3},{4,6},{5,7},{8,10},{9,11},{12,14},{13,15},{18,16},{19,... | collective-permute-start | bytes 1881608 | tf_op jit(solution)/shard_map/ppermute | solution.py:125
  538.0 7.9 %collective-permute-start.56 = (f32[70,2240]{1,0:T(8,128)}, f32[70,2240]{1,0:T(8,128)}, u32[]{:S(2)}, u32[]{:S(2)}) collective-permute-start(f32[70,2240]{1,0:T(8,128)} %slice_select_fusion.1), channel_id=1, source_target_pairs={{0,2},{1,3},{4,6},{5,7},{8,10},{9,11},{12,14},{13,15},{18,16},{19,... | collective-permute-start | bytes 1881608 | tf_op jit(solution)/shard_map/ppermute | solution.py:125
  (53 other events, 203.7 us)
Sparse Core Ops, SparseCore 0:
  284.9 58.4 all-gather.3
